TPU v7x, 32 devices: a whole 2x2x4 slice. The times are simulated.
32 devices in a mesh: outer: 8 (over z, core), inner: 4 (over y, x).
Axes of the slice: x: 2, y: 2, z: 4, core: 2. Of those that a mesh axis runs over, the one named last changes fastest.
Arguments:
- leaf_blocks: float32 [32, 512, 512], P(('outer', 'inner')), as said below
- leaf_bases: float32 [32, 512, 256], P(('outer', 'inner'))
- local_gens: float32 [32, 2, 256, 256], P(('outer', 'inner'))
- chain_gens: float32 [64, 2, 256, 256], P(('outer', 'inner')), as said below
- node_ranks: int32 [3, 32], replicated, may hold values from 192 to 256, as said below
Outputs:
- local_reduced: float32 [32, 256, 256], P(('outer', 'inner'))
- chain_reduced: float32 [64, 256, 256], P(('outer', 'inner'))
- top_factor: float32 [16384, 512], P(('outer', 'inner'))
Inputs may be any that keep to these rules, and one draw needn't show every extreme that they name: `node_ranks`: ranks of all tree levels, entry [v, k] read for k < 32 >> v; both ends of the range occur in every draw. `leaf_blocks`: each leaf block is symmetric positive definite. Rows of chain_gens that belong to the same node are equal on all devices below that node.
All inputs are finite; a program needn't handle non-finite values.
Results may differ from a plain program's by a relative error of at most 0.00017.
Values sent between devices are 32-bit elements; how exact they have to be, the bound alone decides.
A program may use at most 128 MiB of HBM per device.

v0:
```python
import functools

import jax
import jax.numpy as jnp
from jax import lax
from jax.experimental import pallas as pl
from jax.experimental.pallas import tpu as pltpu
from jax.sharding import PartitionSpec as P

LANES = 128
SUB = 8
PANEL = 32
HIGH = lax.Precision.HIGHEST


def dot(a, b, dims=((1,), (0,))):
    return lax.dot_general(a, b, (dims, ((), ())), precision=HIGH, preferred_element_type=jnp.float32)


NT = ((1,), (1,))
TN = ((0,), (0,))


def thirds(x):
    a = x.astype(jnp.bfloat16)
    x = x - a.astype(jnp.float32)
    b = x.astype(jnp.bfloat16)
    return a, b, (x - b.astype(jnp.float32)).astype(jnp.bfloat16)


def bdot(a, b):
    return jnp.dot(a, b, preferred_element_type=jnp.float32)


def iota(shape, axis):
    return lax.broadcasted_iota(jnp.int32, shape, axis)


def total(terms):
    while len(terms) > 1:
        terms = [a + b for a, b in zip(terms[::2], terms[1::2])]
    return terms[0]


def row_of(x, j):
    return jnp.broadcast_to(x[j : j + 1, :], x.shape)


def col_of(x, c):
    return jnp.broadcast_to(x[:, c : c + 1], x.shape)


def eliminate(a_ref, keep_ref=None, reverse=False):
    n = a_ref.shape[0]
    tiles = n // LANES
    groups = PANEL // SUB
    sub = iota((SUB, LANES), 0)
    lane = iota((SUB, LANES), 1)
    wide = iota((n, LANES), 1)

    def order(count):
        return range(count - 1, -1, -1) if reverse else range(count)

    def tile_step(step, carry):
        h = tiles - 1 - step if reverse else step
        own_at = pl.multiple_of(h * LANES, LANES)
        spots = [own_at] + [pl.multiple_of(lax.rem(h + t, tiles) * LANES, LANES) for t in range(1, tiles)]
        ahead = None
        panels = list(order(LANES // PANEL))
        for q in panels:
            base_row = pl.multiple_of(h * LANES + q * PANEL, PANEL)
            rows = [
                [a_ref[pl.ds(pl.multiple_of(base_row + g * SUB, SUB), SUB), pl.ds(spot, LANES)] for spot in spots]
                for g in range(groups)
            ] if ahead is None else ahead
            for s in order(groups):
                c0 = q * PANEL + s * SUB
                cols = [col_of(rows[s][0], c0 + j) for j in range(SUB)]
                other = {g: [col_of(rows[g][0], c0 + j) for j in range(SUB)] for g in range(groups) if g != s}
                piv = list(rows[s])
                kept = [jnp.zeros((SUB, LANES), jnp.float32) for _ in spots]
                left = list(order(SUB))
                inv = 1.0 / row_of(cols[left[0]], left[0])
                while left:
                    j = left.pop(0)
                    here = lane == c0 + j
                    at = sub == j
                    lines = [row_of(x, j) for x in piv]
                    if keep_ref is not None:
                        root = lax.rsqrt(row_of(cols[j], j))
                        kept = [jnp.where(at, x * root, k) for x, k in zip(lines, kept)]
                    mult = jnp.where(at, -1.0, cols[j])
                    now = inv
                    if left:
                        i = left[0]
                        cross = row_of(cols[i], j)
                        inv = 1.0 / (row_of(cols[i], i) - (cross * now) * row_of(cols[j], i))
                    lines = [jnp.where(here, 1.0, lines[0])] + lines[1:]
                    bases = [jnp.where(at | here, 0.0, piv[0])] + [jnp.where(at, 0.0, x) for x in piv[1:]]
                    piv = [y - mult * (x * now) for x, y in zip(lines, bases)]
                    for i in left:
                        cols[i] = jnp.where(at, 0.0, cols[i]) - mult * (row_of(cols[i], j) * now)
                rows[s] = piv
                if keep_ref is not None:
                    for spot, k in zip(spots, kept):
                        keep_ref[pl.ds(pl.multiple_of(base_row + s * SUB, SUB), SUB), pl.ds(spot, LANES)] = k
                spread = [[row_of(x, j) for j in range(SUB)] for x in piv]
                inside = (lane >= c0) & (lane < c0 + SUB)
                for g, mult in other.items():
                    new = list(rows[g])
                    new[0] = jnp.where(inside, 0.0, new[0])
                    rows[g] = [x - total([mult[j] * y[j] for j in range(SUB)]) for x, y in zip(new, spread)]
            weights = []
            for t in range(tiles):
                r1, r2, r3 = thirds(jnp.concatenate([rows[g][t] for g in range(groups)], axis=0))
                blank = jnp.zeros((LANES - 2 * PANEL, LANES), jnp.bfloat16)
                weights.append(jnp.concatenate([r1, r1, r2, r2, r1, r3, blank], axis=0))

            def updated(at, count):
                inside = (wide[:count] >= q * PANEL) & (wide[:count] < (q + 1) * PANEL)
                own = a_ref[pl.ds(at, count), pl.ds(own_at, LANES)]
                olds = [jnp.where(inside, 0.0, own)] + [a_ref[pl.ds(at, count), pl.ds(spot, LANES)] for spot in spots[1:]]
                x = jnp.where(inside, own, 0.0)
                x = x + pltpu.roll(x, PANEL, 1)
                x = x + pltpu.roll(x, 2 * PANEL, 1)
                l1 = x.astype(jnp.bfloat16).astype(jnp.float32)
                l2 = (x - l1).astype(jnp.bfloat16).astype(jnp.float32)
                l3 = x - l1 - l2
                at_quarter = wide[:count] // PANEL
                one = jnp.where((at_quarter & 1) == 0, l1, l2)
                two = jnp.where(at_quarter == 0, l3, jnp.where(at_quarter == 1, l1, 0.0))
                lhs = jnp.concatenate([one.astype(jnp.bfloat16), two.astype(jnp.bfloat16)], axis=1)
                return [old - bdot(lhs, w) for old, w in zip(olds, weights)]

            ahead = None
            if q != panels[-1]:
                onward = -PANEL if reverse else PANEL
                block = updated(pl.multiple_of(base_row + onward, PANEL), PANEL)
                ahead = [[x[g * SUB : (g + 1) * SUB] for x in block] for g in range(groups)]
            for spot, x in zip(spots, updated(0, n)):
                a_ref[:, pl.ds(spot, LANES)] = x
            for g in range(groups):
                for spot, x in zip(spots, rows[g]):
                    a_ref[pl.ds(pl.multiple_of(base_row + g * SUB, SUB), SUB), pl.ds(spot, LANES)] = x
        return carry

    lax.fori_loop(0, tiles, tile_step, 0)


def unit_rest(n, rank):
    return jnp.where((iota((n, n), 0) == iota((n, n), 1)) & (iota((n, n), 0) >= rank), 1.0, 0.0)


def both(n, rank_row, rank_col, x):
    return jnp.where((iota((n, n), 0) < rank_row) & (iota((n, n), 1) < rank_col), x, 0.0)


def place():
    return lax.axis_index("outer") * lax.axis_size("inner") + lax.axis_index("inner")


def leaf_kernel(rank_ref, m_ref, v_ref, g_ref, a_ref):
    n = g_ref.shape[0]
    rank = rank_ref[0, place()]
    keep = iota((n, n), 1) < rank
    v1 = jnp.where(keep, v_ref[:n, :], 0.0)
    v2 = jnp.where(keep, v_ref[n:, :], 0.0)
    a_ref[...] = m_ref[n:, n:]
    eliminate(a_ref)
    m12 = m_ref[:n, n:]
    w = dot(m12, a_ref[...])
    t = dot(a_ref[...], v2)
    a_ref[...] = m_ref[:n, :n] - dot(w, m12, NT)
    y = v1 - dot(w, v2)
    eliminate(a_ref)
    g_ref[...] = dot(v2, t, TN) + dot(y, dot(a_ref[...], y), TN) + unit_rest(n, rank)


def invert_kernel(depth, rank_ref, g_ref, l_ref, a_ref):
    n = g_ref.shape[0]
    rank = rank_ref[depth, jnp.right_shift(place(), depth)]
    a_ref[...] = g_ref[...]
    eliminate(a_ref)
    l_ref[...] = both(n, rank, rank, a_ref[...])


def last_kernel(depth, rank_ref, g_ref, l_ref, e_ref, a_ref):
    n = g_ref.shape[0]
    rank = rank_ref[depth, jnp.right_shift(place(), depth)]
    a_ref[...] = g_ref[...]
    eliminate(a_ref, e_ref, reverse=True)
    l_ref[...] = both(n, rank, rank, a_ref[...])


def merge_kernel(depth, rank_ref, l_ref, gy_ref, mine_ref, theirs_ref, g_ref, a_ref):
    n = g_ref.shape[0]
    node = jnp.right_shift(place(), depth)
    rx, ry = rank_ref[depth, node], rank_ref[depth, jnp.bitwise_xor(node, 1)]
    rp = rank_ref[depth + 1, jnp.right_shift(node, 1)]
    couple = both(n, rx, ry, mine_ref[1] + theirs_ref[1].T)
    px = both(n, rx, rp, mine_ref[0])
    py = both(n, ry, rp, theirs_ref[0])
    gy = gy_ref[...]
    w = dot(couple, gy)
    a_ref[...] = l_ref[...] + unit_rest(n, rx) - dot(w, couple, NT)
    y = px - dot(w, py)
    t = dot(py, dot(gy, py), TN)
    eliminate(a_ref)
    g_ref[...] = t + dot(y, dot(a_ref[...], y), TN) + unit_rest(n, rp)


def top_kernel(depth, rank_ref, l_ref, e_ref, lo_ref, eo_ref, c_ref, co_ref, f_ref, a_ref, keep_ref):
    n = l_ref.shape[0]
    pos = lax.axis_index("outer")
    first = jnp.bitwise_and(pos, 1) == 0
    node = jnp.bitwise_and(pos, -2)
    ra, rb = rank_ref[depth, node], rank_ref[depth, node + 1]
    row, col = iota((n, n), 0), iota((n, n), 1)
    pick = jnp.where(first, 1, 0) + jnp.zeros((n, n), jnp.int32) > 0
    ca = jnp.where(pick, c_ref[...], co_ref[...])
    cb = jnp.where(pick, co_ref[...], c_ref[...])
    lb = jnp.where(pick, lo_ref[...], l_ref[...])
    e = jnp.where(pick, e_ref[...], eo_ref[...])
    couple = both(n, ra, rb, ca + cb.T)
    f21 = dot(couple, jnp.where(row >= col, e, 0.0), ((0,), (1,)))
    a_ref[...] = lb + unit_rest(n, rb) - dot(f21, f21, NT)
    eliminate(a_ref, keep_ref)
    upper = jnp.where(row < col, e, 0.0) + jnp.where(row == col, 1.0 / jnp.where(row == col, e, 1.0), 0.0)
    f_ref[:n, :n] = upper.T
    f_ref[:n, n:] = jnp.zeros((n, n), jnp.float32)
    f_ref[n:, :n] = f21
    f_ref[n:, n:] = jnp.where(row <= col, keep_ref[...], 0.0).T


def call(kernel, name, outs, n, ranks, *arrays, keep=False):
    vmem = pl.BlockSpec(memory_space=pltpu.VMEM)
    square = pltpu.VMEM((n, n), jnp.float32)
    return pl.pallas_call(
        kernel,
        name=name,
        out_shape=[jax.ShapeDtypeStruct(shape, jnp.float32) for shape in outs],
        in_specs=[pl.BlockSpec(memory_space=pltpu.SMEM)] + [vmem] * len(arrays),
        out_specs=[vmem] * len(outs),
        scratch_shapes=[square] * (2 if keep else 1),
        cost_estimate=pl.CostEstimate(flops=4 * 10**9, bytes_accessed=4 * 10**6, transcendentals=0),
    )(ranks, *arrays)


def partner(x, axis, bit):
    return lax.ppermute(x, axis, [(i, i ^ 1 << bit) for i in range(lax.axis_size(axis))])


def body(leaf_blocks, leaf_bases, local_gens, chain_gens, node_ranks):
    n = leaf_bases.shape[2]
    in_levels = chain_gens.shape[0]
    square = (n, n)
    gens = [local_gens[0]] + [chain_gens[d] for d in range(in_levels)]
    others = [partner(gens[d], "inner", d) for d in range(in_levels)]
    couple = gens[in_levels][1]
    other_couple = partner(couple, "outer", 0)
    g = call(leaf_kernel, "leaf", [square], n, node_ranks, leaf_blocks[0], leaf_bases[0])[0]
    reduced = []
    for depth in range(in_levels):
        g_other = partner(g, "inner", depth)
        mine = call(functools.partial(invert_kernel, depth), "invert", [square], n, node_ranks, g)[0]
        reduced.append(mine)
        merge = functools.partial(merge_kernel, depth)
        g = call(merge, "merge", [square], n, node_ranks, mine, g_other, gens[depth], others[depth])[0]
    last = functools.partial(last_kernel, in_levels)
    mine, roots = call(last, "last", [square, square], n, node_ranks, g)
    reduced.append(mine)
    other_mine, other_roots = partner((mine, roots), "outer", 0)
    top = functools.partial(top_kernel, in_levels)
    arrays = (mine, roots, other_mine, other_roots, couple, other_couple)
    factor = call(top, "top", [(2 * n, 2 * n)], n, node_ranks, *arrays, keep=True)[0]
    return (reduced[0][None], jnp.stack(reduced[1:], axis=0), factor)


def solution(mesh):
    return jax.shard_map(
        body,
        mesh=mesh,
        in_specs=(
            P(("outer", "inner"), None, None),
            P(("outer", "inner"), None, None),
            P(("outer", "inner"), None, None, None),
            P(("outer", "inner"), None, None, None),
            P(),
        ),
        out_specs=(
            P(("outer", "inner"), None, None),
            P(("outer", "inner"), None, None),
            P(("outer", "inner"), None),
        ),
        check_vma=False,
    )
```

profile of v0, /device:TPU:0, one launch (start us, length us, event | category | flops | bytes accessed | tf_op | source)
XLA Modules:
  0.0 118.4 jit_solution(14497284160647017352)
XLA Ops:
  0.6 0.0 copy-start.4
  0.7 24.0 %leaf.1.g_ref = f32[256,256]{1,0:T(8,128)} custom-call(s32[3,32]{1,0:T(4,128)} %rank_ref.13, f32[512,512]{1,0:T(8,128)} %bitcast.12, f32[512,256]{1,0:T(8,128)} %bitcast.13), custom_call_target="tpu_custom_call" | custom-call | flops 4000000000 | bytes 4000000 | tf_op jit(solution)/shard_map/leaf/pallas_call | solution.py:238
  24.7 3.0 %collective-permute-start = (f32[256,256]{1,0:T(8,128)}, f32[256,256]{1,0:T(8,128)}, u32[]{:S(2)}, u32[]{:S(2)}) collective-permute-start(f32[256,256]{1,0:T(8,128)} %leaf.1.g_ref), channel_id=1, source_target_pairs={{0,1},{1,0},{2,3},{3,2},{4,5},{5,4},{6,7},{7,6},{8,9},{9,8},{10,11... | collective-permute-start | bytes 786440 | tf_op jit(solution)/shard_map/ppermute | solution.py:250
  27.6 0.0 collective-permute-start.1
  27.7 0.0 copy-start.1
  27.7 2.1 %collective-permute-start.3 = (f32[2,256,256]{2,1,0:T(8,128)S(1)}, f32[2,256,256]{2,1,0:T(8,128)S(1)}, u32[]{:S(2)}, u32[]{:S(2)}) collective-permute-start(f32[2,256,256]{2,1,0:T(8,128)S(1)} %slice_bitcast_fusion.mine_ref), channel_id=1, source_target_pairs={{0,2},{1,3},{2,0},{3,1},{4,6},{5,7},{6,4},{7,5},{8,10},{9,11},{10,... | collective-permute-start | bytes 1572872 | tf_op jit(solution)/shard_map/ppermute | solution.py:250
  29.8 0.1 collective-permute-start.6
  29.9 11.4 %invert.2.l_ref = f32[256,256]{1,0:T(8,128)} custom-call(s32[3,32]{1,0:T(4,128)} %rank_ref.13, f32[256,256]{1,0:T(8,128)} %leaf.1.g_ref), custom_call_target="tpu_custom_call" | custom-call | flops 4000000000 | bytes 4000000 | tf_op jit(solution)/shard_map/invert/pallas_call | solution.py:238
  41.3 4.1 %collective-permute-done.1.theirs_ref = f32[2,256,256]{2,1,0:T(8,128)S(1)} collective-permute-done((f32[2,256,256]{2,1,0:T(8,128)S(1)}, f32[2,256,256]{2,1,0:T(8,128)S(1)}, u32[]{:S(2)}, u32[]{:S(2)}) %collective-permute-start.1) | collective-permute-done | bytes 524320 | tf_op jit(solution)/shard_map/ppermute | solution.py:250
  45.4 0.8 copy-done.6
  46.2 14.7 %merge.2.g_ref = f32[256,256]{1,0:T(8,128)} custom-call(s32[3,32]{1,0:T(4,128)} %rank_ref.13, f32[256,256]{1,0:T(8,128)} %invert.2.l_ref, f32[256,256]{1,0:T(8,128)} %collective-permute-done.gy_ref, f32[2,256,256]{2,1,0:T(8,128)} %bitcast.14, f32[2,256,256]{2,1,0:T(8,128)} %copy-done.6), custom_call_target="tpu_custom_call" | custom-call | flops 4000000000 | bytes 4000000 | tf_op jit(solution)/shard_map/merge/pallas_call | solution.py:238
  60.9 1.8 %collective-permute-start.2 = (f32[256,256]{1,0:T(8,128)}, f32[256,256]{1,0:T(8,128)S(1)}, u32[]{:S(2)}, u32[]{:S(2)}) collective-permute-start(f32[256,256]{1,0:T(8,128)} %merge.2.g_ref), channel_id=1, source_target_pairs={{0,2},{1,3},{2,0},{3,1},{4,6},{5,7},{6,4},{7,5},{8,10},{9,11},{10,... | collective-permute-start | bytes 786440 | tf_op jit(solution)/shard_map/ppermute | solution.py:250
  62.6 11.4 %invert.3.l_ref = f32[256,256]{1,0:T(8,128)} custom-call(s32[3,32]{1,0:T(4,128)} %rank_ref.13, f32[256,256]{1,0:T(8,128)} %merge.2.g_ref), custom_call_target="tpu_custom_call" | custom-call | flops 4000000000 | bytes 4000000 | tf_op jit(solution)/shard_map/invert/pallas_call | solution.py:238
  74.0 0.0 collective-permute-done.3.theirs_ref
  74.1 0.8 copy-done.5
  74.8 0.7 copy-done.10
  75.5 14.5 %merge.3.g_ref = f32[256,256]{1,0:T(8,128)} custom-call(s32[3,32]{1,0:T(4,128)} %rank_ref.13, f32[256,256]{1,0:T(8,128)} %invert.3.l_ref, f32[256,256]{1,0:T(8,128)} %copy-done.10, f32[2,256,256]{2,1,0:T(8,128)} %copy-done.1, f32[2,256,256]{2,1,0:T(8,128)} %copy-done.5), custom_call_target="tpu_custom_call" | custom-call | flops 4000000000 | bytes 4000000 | tf_op jit(solution)/shard_map/merge/pallas_call | solution.py:238
  90.1 11.2 %last.1 = (f32[256,256]{1,0:T(8,128)}, f32[256,256]{1,0:T(8,128)}) custom-call(s32[3,32]{1,0:T(4,128)} %rank_ref.13, f32[256,256]{1,0:T(8,128)} %merge.3.g_ref), custom_call_target="tpu_custom_call" | custom-call | flops 4000000000 | bytes 4000000 | tf_op jit(solution)/shard_map/last/pallas_call | solution.py:238
  101.2 0.5 collective-permute-start.5
  101.8 1.8 %pad_maximum_fusion = f32[2,256,256]{2,1,0:T(8,128)} fusion(f32[1,256,256]{2,1,0:T(8,128)} %bitcast.11, f32[1,256,256]{2,1,0:T(8,128)S(1)} %bitcast.10), kind=kLoop, calls=%fused_computation | loop fusion | flops 131072 | bytes 1048576 | tf_op jit(solution)/shard_map/stack | solution.py:276
  103.6 0.7 copy-done.7
  104.2 0.1 copy-done.8
  104.3 0.7 copy-done.9
  105.0 13.4 %top.1 = f32[512,512]{1,0:T(8,128)} custom-call(s32[3,32]{1,0:T(4,128)} %rank_ref.13, f32[256,256]{1,0:T(8,128)} %get-tuple-element.5.l_ref, f32[256,256]{1,0:T(8,128)} %get-tuple-element.6.e_ref, f32[256,256]{1,0:T(8,128)} %copy-done.8, f32[256,256]{1,0:T(8,128)} %copy-done.9, f32[256,256]{1,0:T(8,128)} %copy-done.2, f32[256,256]{1,0:T(8,128)} %copy-done.7), custom_call_target="tpu_custom_call" | custom-call | flops 4000000000 | bytes 4000000 | tf_op jit(solution)/shard_map/top/pallas_call | solution.py:238
  (22 shorter events, 0.1 us)
Async XLA Ops:
  0.6 27.0 %copy-start.4 = (f32[1,2,256,256]{3,2,1,0:T(8,128)S(1)}, f32[1,2,256,256]{3,2,1,0:T(8,128)}, u32[]{:S(2)}) copy-start(f32[1,2,256,256]{3,2,1,0:T(8,128)} %param.7) | copy-start | bytes 1572868
  0.6 27.0 %copy-start = (f32[2,2,256,256]{3,2,1,0:T(8,128)S(1)}, f32[2,2,256,256]{3,2,1,0:T(8,128)}, u32[]{:S(2)}) copy-start(f32[2,2,256,256]{3,2,1,0:T(8,128)} %param.8) | copy-start | bytes 3145732
  24.7 16.6 %collective-permute-start = (f32[256,256]{1,0:T(8,128)}, f32[256,256]{1,0:T(8,128)}, u32[]{:S(2)}, u32[]{:S(2)}) collective-permute-start(f32[256,256]{1,0:T(8,128)} %leaf.1.g_ref), channel_id=1, source_target_pairs={{0,1},{1,0},{2,3},{3,2},{4,5},{5,4},{6,7},{7,6},{8,9},{9,8},{10,11... | collective-permute-start | bytes 786440 | tf_op jit(solution)/shard_map/ppermute | solution.py:250
  27.6 17.7 %collective-permute-start.1 = (f32[2,256,256]{2,1,0:T(8,128)S(1)}, f32[2,256,256]{2,1,0:T(8,128)S(1)}, u32[]{:S(2)}, u32[]{:S(2)}) collective-permute-start(f32[2,256,256]{2,1,0:T(8,128)S(1)} %bitcast.15), channel_id=1, source_target_pairs={{0,1},{1,0},{2,3},{3,2},{4,5},{5,4},{6,7},{7,6},{8,9},{9,8},{10,11... | collective-permute-start | bytes 1572872 | tf_op jit(solution)/shard_map/ppermute | solution.py:250
  27.7 13.6 %copy-start.1 = (f32[2,256,256]{2,1,0:T(8,128)}, f32[2,256,256]{2,1,0:T(8,128)S(1)}, u32[]{:S(2)}) copy-start(f32[2,256,256]{2,1,0:T(8,128)S(1)} %slice_bitcast_fusion.mine_ref) | copy-start | bytes 1572868
  27.7 46.4 %collective-permute-start.3 = (f32[2,256,256]{2,1,0:T(8,128)S(1)}, f32[2,256,256]{2,1,0:T(8,128)S(1)}, u32[]{:S(2)}, u32[]{:S(2)}) collective-permute-start(f32[2,256,256]{2,1,0:T(8,128)S(1)} %slice_bitcast_fusion.mine_ref), channel_id=1, source_target_pairs={{0,2},{1,3},{2,0},{3,1},{4,6},{5,7},{6,4},{7,5},{8,10},{9,11},{10,... | collective-permute-start | bytes 1572872 | tf_op jit(solution)/shard_map/ppermute | solution.py:250
  29.8 11.5 %copy-start.2 = (f32[256,256]{1,0:T(8,128)}, f32[256,256]{1,0:T(8,128)S(1)}, u32[]{:S(2)}) copy-start(f32[256,256]{1,0:T(8,128)S(1)} %slice_bitcast_fusion.1.c_ref) | copy-start | bytes 786436
  29.8 73.7 %collective-permute-start.6 = (f32[256,256]{1,0:T(8,128)S(1)}, f32[256,256]{1,0:T(8,128)S(1)}, u32[]{:S(2)}, u32[]{:S(2)}) collective-permute-start(f32[256,256]{1,0:T(8,128)S(1)} %slice_bitcast_fusion.1.c_ref), channel_id=1, source_target_pairs={{0,4},{4,0},{8,12},{12,8},{16,20},{20,16},{24,28},{28,24},{1,5},{5... | collective-permute-start | bytes 786440 | tf_op jit(solution)/shard_map/ppermute | solution.py:250
  45.4 0.8 copy-start.6
  60.9 13.2 %collective-permute-start.2 = (f32[256,256]{1,0:T(8,128)}, f32[256,256]{1,0:T(8,128)S(1)}, u32[]{:S(2)}, u32[]{:S(2)}) collective-permute-start(f32[256,256]{1,0:T(8,128)} %merge.2.g_ref), channel_id=1, source_target_pairs={{0,2},{1,3},{2,0},{3,1},{4,6},{5,7},{6,4},{7,5},{8,10},{9,11},{10,... | collective-permute-start | bytes 786440 | tf_op jit(solution)/shard_map/ppermute | solution.py:250
  74.0 0.8 copy-start.5
  74.8 0.7 copy-start.10
  90.1 11.7 %copy-start.3 = (f32[256,256]{1,0:T(8,128)S(1)}, f32[256,256]{1,0:T(8,128)}, u32[]{:S(2)}) copy-start(f32[256,256]{1,0:T(8,128)} %invert.3.l_ref) | copy-start | bytes 786436
  101.2 2.3 %collective-permute-start.4 = (f32[256,256]{1,0:T(8,128)}, f32[256,256]{1,0:T(8,128)S(1)}, u32[]{:S(2)}, u32[]{:S(2)}) collective-permute-start(f32[256,256]{1,0:T(8,128)} %get-tuple-element.5.l_ref), channel_id=1, source_target_pairs={{0,4},{4,0},{8,12},{12,8},{16,20},{20,16},{24,28},{28,24},{1,5},{5... | collective-permute-start | bytes 786440 | tf_op jit(solution)/shard_map/ppermute | solution.py:250
  101.2 2.3 %collective-permute-start.5 = (f32[256,256]{1,0:T(8,128)}, f32[256,256]{1,0:T(8,128)S(1)}, u32[]{:S(2)}, u32[]{:S(2)}) collective-permute-start(f32[256,256]{1,0:T(8,128)} %get-tuple-element.6.e_ref), channel_id=1, source_target_pairs={{0,4},{4,0},{8,12},{12,8},{16,20},{20,16},{24,28},{28,24},{1,5},{5... | collective-permute-start | bytes 786440 | tf_op jit(solution)/shard_map/ppermute | solution.py:250
  103.5 0.7 copy-start.7
  103.5 0.8 copy-start.8
  104.3 0.7 copy-start.9
where the time goes:
time: 119 us; the launch traced here: 118 us
  Pallas kernels  101 us (85%)
  starting transfers between devices  7.44 us (6%)
  waiting for transfers between devices  4.08 us (3%)
  local copies, waits for them, and re-layouts  3.84 us (3%)
  other arithmetic  1.78 us (1%)
    pallas_call x7, Pallas kernels, call(): pl.pallas_call(kernel, name=name, out_shape=[jax.ShapeDtypeStruct(shape,...  101 us
    ppermute x7, starting transfers between devices, partner(): lax.ppermute(x, axis, [(i, i ^ 1 << bit) for i in range(lax.axis_size(axi...  7.44 us
    ppermute x7, waiting for transfers between devices, partner(): lax.ppermute(x, axis, [(i, i ^ 1 << bit) for i in range(lax.axis_size(axi...  4.08 us
    unnamed x22, local copies, waits for them, and re-layouts  3.79 us
  transfers between devices with their start and end apart: 7, of which 1 were waited for; matrix products, arithmetic and copies ran while one was open for 2% of the time, Pallas kernels for 53%

commit v1 on v0

v1 whole, which is shorter than its diff:
```python
import functools

import jax
import jax.numpy as jnp
from jax import lax
from jax.experimental import pallas as pl
from jax.experimental.pallas import tpu as pltpu
from jax.sharding import PartitionSpec as P

LANES = 128
SUB = 8
PANEL = 32
TOLERANCE = 4e-6
MOST = 40
HIGH = lax.Precision.HIGHEST


def dot(a, b, dims=((1,), (0,))):
    return lax.dot_general(a, b, (dims, ((), ())), precision=HIGH, preferred_element_type=jnp.float32)


NT = ((1,), (1,))
TN = ((0,), (0,))


def thirds(x):
    a = x.astype(jnp.bfloat16)
    x = x - a.astype(jnp.float32)
    b = x.astype(jnp.bfloat16)
    return a, b, (x - b.astype(jnp.float32)).astype(jnp.bfloat16)


def bdot(a, b):
    return jnp.dot(a, b, preferred_element_type=jnp.float32)


def iota(shape, axis):
    return lax.broadcasted_iota(jnp.int32, shape, axis)


def total(terms):
    while len(terms) > 1:
        terms = [a + b for a, b in zip(terms[::2], terms[1::2])]
    return terms[0]


def row_of(x, j):
    return jnp.broadcast_to(x[j : j + 1, :], x.shape)


def col_of(x, c):
    return jnp.broadcast_to(x[:, c : c + 1], x.shape)


def tile_pass(a_ref, keep_ref, reverse, h):
    n = a_ref.shape[0]
    tiles = n // LANES
    groups = PANEL // SUB
    sub = iota((SUB, LANES), 0)
    lane = iota((SUB, LANES), 1)
    wide = iota((n, LANES), 1)

    def order(count):
        return range(count - 1, -1, -1) if reverse else range(count)

    own_at = pl.multiple_of(h * LANES, LANES)
    spots = [own_at] + [pl.multiple_of(lax.rem(h + t, tiles) * LANES, LANES) for t in range(1, tiles)]
    ahead = None
    panels = list(order(LANES // PANEL))
    for q in panels:
        base_row = pl.multiple_of(h * LANES + q * PANEL, PANEL)
        rows = [
            [a_ref[pl.ds(pl.multiple_of(base_row + g * SUB, SUB), SUB), pl.ds(spot, LANES)] for spot in spots]
            for g in range(groups)
        ] if ahead is None else ahead
        for s in order(groups):
            c0 = q * PANEL + s * SUB
            cols = [col_of(rows[s][0], c0 + j) for j in range(SUB)]
            other = {g: [col_of(rows[g][0], c0 + j) for j in range(SUB)] for g in range(groups) if g != s}
            piv = list(rows[s])
            kept = [jnp.zeros((SUB, LANES), jnp.float32) for _ in spots]
            left = list(order(SUB))
            inv = 1.0 / row_of(cols[left[0]], left[0])
            yield
            while left:
                j = left.pop(0)
                here = lane == c0 + j
                at = sub == j
                lines = [row_of(x, j) for x in piv]
                if keep_ref is not None:
                    root = lax.rsqrt(row_of(cols[j], j))
                    kept = [jnp.where(at, x * root, k) for x, k in zip(lines, kept)]
                mult = jnp.where(at, -1.0, cols[j])
                now = inv
                if left:
                    i = left[0]
                    cross = row_of(cols[i], j)
                    inv = 1.0 / (row_of(cols[i], i) - (cross * now) * row_of(cols[j], i))
                lines = [jnp.where(here, 1.0, lines[0])] + lines[1:]
                bases = [jnp.where(at | here, 0.0, piv[0])] + [jnp.where(at, 0.0, x) for x in piv[1:]]
                piv = [y - mult * (x * now) for x, y in zip(lines, bases)]
                for i in left:
                    cols[i] = jnp.where(at, 0.0, cols[i]) - mult * (row_of(cols[i], j) * now)
                yield
            rows[s] = piv
            if keep_ref is not None:
                for spot, k in zip(spots, kept):
                    keep_ref[pl.ds(pl.multiple_of(base_row + s * SUB, SUB), SUB), pl.ds(spot, LANES)] = k
            spread = [[row_of(x, j) for j in range(SUB)] for x in piv]
            inside = (lane >= c0) & (lane < c0 + SUB)
            for g, mult in other.items():
                new = list(rows[g])
                new[0] = jnp.where(inside, 0.0, new[0])
                rows[g] = [x - total([mult[j] * y[j] for j in range(SUB)]) for x, y in zip(new, spread)]
                yield
        weights = []
        for t in range(tiles):
            r1, r2, r3 = thirds(jnp.concatenate([rows[g][t] for g in range(groups)], axis=0))
            blank = jnp.zeros((LANES - 2 * PANEL, LANES), jnp.bfloat16)
            weights.append(jnp.concatenate([r1, r1, r2, r2, r1, r3, blank], axis=0))
        yield

        def updated(at, count):
            inside = (wide[:count] >= q * PANEL) & (wide[:count] < (q + 1) * PANEL)
            own = a_ref[pl.ds(at, count), pl.ds(own_at, LANES)]
            olds = [jnp.where(inside, 0.0, own)] + [a_ref[pl.ds(at, count), pl.ds(spot, LANES)] for spot in spots[1:]]
            x = jnp.where(inside, own, 0.0)
            x = x + pltpu.roll(x, PANEL, 1)
            x = x + pltpu.roll(x, 2 * PANEL, 1)
            l1 = x.astype(jnp.bfloat16).astype(jnp.float32)
            l2 = (x - l1).astype(jnp.bfloat16).astype(jnp.float32)
            l3 = x - l1 - l2
            at_quarter = wide[:count] // PANEL
            one = jnp.where((at_quarter & 1) == 0, l1, l2)
            two = jnp.where(at_quarter == 0, l3, jnp.where(at_quarter == 1, l1, 0.0))
            lhs = jnp.concatenate([one.astype(jnp.bfloat16), two.astype(jnp.bfloat16)], axis=1)
            return [old - bdot(lhs, w) for old, w in zip(olds, weights)]

        ahead = None
        if q != panels[-1]:
            onward = -PANEL if reverse else PANEL
            block = updated(pl.multiple_of(base_row + onward, PANEL), PANEL)
            ahead = [[x[g * SUB : (g + 1) * SUB] for x in block] for g in range(groups)]
        yield
        for spot, x in zip(spots, updated(0, n)):
            a_ref[:, pl.ds(spot, LANES)] = x
        for g in range(groups):
            for spot, x in zip(spots, rows[g]):
                a_ref[pl.ds(pl.multiple_of(base_row + g * SUB, SUB), SUB), pl.ds(spot, LANES)] = x
        yield


def together(passes):
    while passes:
        passes = [p for p in passes if next(p, passes) is not passes]


def eliminate(refs, keeps=None, reverse=False):
    tiles = refs[0].shape[0] // LANES
    keeps = keeps or [None] * len(refs)

    def step(i, carry):
        h = tiles - 1 - i if reverse else i
        together([tile_pass(a, k, reverse, h) for a, k in zip(refs, keeps)])
        return carry

    lax.fori_loop(0, tiles, step, 0)


def unit_rest(n, rank):
    return jnp.where((iota((n, n), 0) == iota((n, n), 1)) & (iota((n, n), 0) >= rank), 1.0, 0.0)


def both(n, rank_row, rank_col, x):
    return jnp.where((iota((n, n), 0) < rank_row) & (iota((n, n), 1) < rank_col), x, 0.0)


def place():
    return lax.axis_index("outer") * lax.axis_size("inner") + lax.axis_index("inner")


def rank_at(rank_ref, depth, flip=0, up=0):
    return rank_ref[depth + up, jnp.bitwise_xor(jnp.right_shift(place(), depth + up), flip)]


def product(a, b, nt=False):
    return lax.dot_general(a, b, (NT if nt else ((1,), (0,)), ((), ())), preferred_element_type=jnp.float32)


def dot6(a, b, nt=False):
    (a1, a2, a3), (b1, b2, b3) = a, b
    axis = 1 if nt else 0
    small = product(jnp.concatenate([a2, a1, a3], axis=1), jnp.concatenate([b2, b3, b1], axis=axis), nt)
    large = product(jnp.concatenate([a2, a1, a1], axis=1), jnp.concatenate([b1, b2, b1], axis=axis), nt)
    return small + large


def dot3(a, b, nt=False):
    axis = 1 if nt else 0
    small = product(jnp.concatenate([a[1], a[0]], axis=1), jnp.concatenate([b[0], b[1]], axis=axis), nt)
    return small + product(a[0], b[0], nt)


def slow_dot(out_ref, a_ref, b_ref, dims=((1,), (0,)), add=False):
    n = out_ref.shape[0]

    def rows(i, carry):
        at = pl.ds(pl.multiple_of(i * PANEL, PANEL), PANEL)
        x = dot(a_ref[at, :], b_ref[...], dims)
        out_ref[at, :] = x + b_ref[at, :] if add else x
        return carry

    lax.fori_loop(0, n // PANEL, rows, 0)


def square_sum(x):
    return jnp.sum(x * x)


def neumann(steps, x_ref, y_ref, s_ref, z, hold_ref, work):
    z_ref, p_ref, q_ref, w_ref = work
    s = thirds(s_ref[...])
    a = dot3(thirds(x_ref[...]), s)
    u = dot3(s, thirds(y_ref[...]))
    power = thirds(dot3(thirds(a), thirds(u), nt=True))
    hold_ref[...] = z
    z = z + dot3(power, thirds(z))
    for _ in range(steps - 1):
        raised = dot3(power, power)
        power = thirds(raised)
        z = z + dot3(power, thirds(z))
    z_ref[...] = z

    @pl.when(square_sum(raised) > TOLERANCE)
    def _():
        slow_dot(p_ref, x_ref, s_ref)
        slow_dot(q_ref, s_ref, y_ref)
        slow_dot(w_ref, p_ref, q_ref, NT)
        z_ref[...] = hold_ref[...]

        def more(carry):
            count, rest = carry
            return (count < MOST) & (rest > TOLERANCE)

        def raise_power(carry):
            count, _ = carry
            slow_dot(p_ref, w_ref, z_ref, add=True)
            z_ref[...] = p_ref[...]
            slow_dot(q_ref, w_ref, w_ref)
            rest = square_sum(w_ref[...])
            w_ref[...] = q_ref[...]
            return count + 1, rest

        lax.while_loop(more, raise_power, (jnp.int32(0), jnp.float32(1.0)))


def combine(steps, x_ref, y_ref, s_ref, px, py, g_ref, work):
    py3 = thirds(py)
    t = thirds(dot6(thirds(y_ref[...]), py3))
    y = px - dot6(thirds(s_ref[...]), t)
    z = dot6(thirds(x_ref[...]), thirds(y))
    g = dot6(thirds(py.T), t)
    turned = y.T
    neumann(steps, x_ref, y_ref, s_ref, z, g_ref, work)
    return g + dot6(thirds(turned), thirds(work[0][...]))


def leaf_kernel(rank_ref, m_ref, v_ref, g_ref, x_ref, y_ref, s_ref, *work):
    n = g_ref.shape[0]
    rank = rank_ref[0, place()]
    keep = iota((n, n), 1) < rank
    x_ref[...] = m_ref[:n, :n]
    y_ref[...] = m_ref[n:, n:]
    s_ref[...] = m_ref[:n, n:]
    eliminate([x_ref, y_ref])
    px = jnp.where(keep, v_ref[:n, :], 0.0)
    py = jnp.where(keep, v_ref[n:, :], 0.0)
    g_ref[...] = combine(3, x_ref, y_ref, s_ref, px, py, g_ref, work) + unit_rest(n, rank)


def merge_kernel(depth, rank_ref, x_ref, y_ref, mine_ref, theirs_ref, g_ref, s_ref, *work):
    n = g_ref.shape[0]
    rx, ry, rp = rank_at(rank_ref, depth), rank_at(rank_ref, depth, 1), rank_at(rank_ref, depth, 0, 1)
    s_ref[...] = both(n, rx, ry, mine_ref[1] + theirs_ref[1].T)
    px = both(n, rx, rp, mine_ref[0])
    py = both(n, ry, rp, theirs_ref[0])
    g_ref[...] = combine(2, x_ref, y_ref, s_ref, px, py, g_ref, work) + unit_rest(n, rp)


def first_kernel(g_ref, half_ref):
    half_ref[...] = g_ref[...]
    together([tile_pass(half_ref, None, False, 0)])


def middle_kernel(depth, rank_ref, before_ref, g_ref, l_ref, half_ref, a_ref):
    n = g_ref.shape[0]
    a_ref[...] = before_ref[...]
    half_ref[...] = g_ref[...]
    together([tile_pass(a_ref, None, False, 1), tile_pass(half_ref, None, False, 0)])
    rank = rank_at(rank_ref, depth - 1)
    l_ref[...] = both(n, rank, rank, a_ref[...])


def final_kernel(depth, rank_ref, before_ref, l_ref, a_ref):
    n = l_ref.shape[0]
    a_ref[...] = before_ref[...]
    together([tile_pass(a_ref, None, False, 1)])
    rank = rank_at(rank_ref, depth - 1)
    l_ref[...] = both(n, rank, rank, a_ref[...])


def factor_of(n, e):
    row, col = iota((n, n), 0), iota((n, n), 1)
    upper = jnp.where(row < col, e, 0.0) + jnp.where(row == col, 1.0 / jnp.where(row == col, e, 1.0), 0.0)
    return upper.T


def top_kernel(depth, rank_ref, g_ref, go_ref, c_ref, co_ref, f_ref, l_ref, a_ref, b_ref, ka_ref, kb_ref, s_ref, *work):
    n = g_ref.shape[0]
    pos = lax.axis_index("outer")
    first = jnp.bitwise_and(pos, 1) == 0
    node = jnp.bitwise_and(pos, -2)
    ra, rb = rank_ref[depth, node], rank_ref[depth, node + 1]
    row, col = iota((n, n), 0), iota((n, n), 1)
    pick = jnp.where(first, 1, 0) + jnp.zeros((n, n), jnp.int32) > 0
    a_ref[...] = jnp.where(pick, g_ref[...], go_ref[...])
    b_ref[...] = jnp.where(pick, go_ref[...], g_ref[...])
    ca = jnp.where(pick, c_ref[...], co_ref[...])
    cb = jnp.where(pick, co_ref[...], c_ref[...])
    s_ref[...] = both(n, rb, ra, ca.T + cb)
    neumann(2, b_ref, a_ref, s_ref, b_ref[...], l_ref, work)
    b_ref[...] = work[0][...]
    back = dot6(thirds(dot6(thirds(s_ref[...]), thirds(a_ref[...]))), thirds(s_ref[...]), nt=True)
    l_ref[...] = back
    eliminate([a_ref, b_ref], [ka_ref, kb_ref], reverse=True)
    e = ka_ref[...]
    rank = jnp.where(first, ra, rb)
    l_ref[...] = both(n, rank, rank, jnp.where(pick, a_ref[...], b_ref[...] + l_ref[...]))
    f_ref[:n, :n] = factor_of(n, e)
    f_ref[:n, n:] = jnp.zeros((n, n), jnp.float32)
    f_ref[n:, :n] = dot6(thirds(s_ref[...]), thirds(jnp.where(row >= col, e, 0.0)), nt=True)
    f_ref[n:, n:] = factor_of(n, kb_ref[...])


def call(kernel, name, outs, n, scratch, *arrays, ranks=None, flops=10**9):
    vmem = pl.BlockSpec(memory_space=pltpu.VMEM)
    lead = [] if ranks is None else [pl.BlockSpec(memory_space=pltpu.SMEM)]
    return pl.pallas_call(
        kernel,
        name=name,
        out_shape=[jax.ShapeDtypeStruct(shape, jnp.float32) for shape in outs],
        in_specs=lead + [vmem] * len(arrays),
        out_specs=[vmem] * len(outs),
        scratch_shapes=[pltpu.VMEM((n, n), jnp.float32)] * scratch,
        cost_estimate=pl.CostEstimate(flops=flops, bytes_accessed=4 * 10**6, transcendentals=0),
    )(*([] if ranks is None else [ranks]), *arrays)


def partner(x, axis, bit):
    return lax.ppermute(x, axis, [(i, i ^ 1 << bit) for i in range(lax.axis_size(axis))])


def body(leaf_blocks, leaf_bases, local_gens, chain_gens, node_ranks):
    n = leaf_bases.shape[2]
    in_levels = chain_gens.shape[0]
    square = (n, n)
    gens = [local_gens[0]] + [chain_gens[d] for d in range(in_levels)]
    others = [partner(gens[d], "inner", d) for d in range(in_levels)]
    couple = gens[in_levels][1]
    other_couple = partner(couple, "outer", 0)
    g = call(leaf_kernel, "leaf", [square], n, 7, leaf_blocks[0], leaf_bases[0], ranks=node_ranks, flops=8 * 10**9)[0]
    reduced = []
    half = None
    for depth in range(in_levels):
        g_other = partner(g, "inner", depth)
        if depth == 0:
            half = call(first_kernel, "first", [square], n, 0, g, flops=4 * 10**9)[0]
        else:
            middle = functools.partial(middle_kernel, depth)
            done, half = call(middle, "middle", [square] * 2, n, 1, half, g, ranks=node_ranks, flops=4 * 10**9)
            reduced.append(done)
        merge = functools.partial(merge_kernel, depth)
        g = call(merge, "merge", [square], n, 5, g, g_other, gens[depth], others[depth], ranks=node_ranks)[0]
    g_other = partner(g, "outer", 0)
    final = functools.partial(final_kernel, in_levels)
    reduced.append(call(final, "final", [square], n, 1, half, ranks=node_ranks, flops=4 * 10**9)[0])
    top = functools.partial(top_kernel, in_levels)
    arrays = (g, g_other, couple, other_couple)
    factor, done = call(top, "top", [(2 * n, 2 * n), square], n, 9, *arrays, ranks=node_ranks, flops=4 * 10**9)
    reduced.append(done)
    return (reduced[0][None], jnp.stack(reduced[1:], axis=0), factor)


def solution(mesh):
    return jax.shard_map(
        body,
        mesh=mesh,
        in_specs=(
            P(("outer", "inner"), None, None),
            P(("outer", "inner"), None, None),
            P(("outer", "inner"), None, None, None),
            P(("outer", "inner"), None, None, None),
            P(),
        ),
        out_specs=(
            P(("outer", "inner"), None, None),
            P(("outer", "inner"), None, None),
            P(("outer", "inner"), None),
        ),
        check_vma=False,
    )
```

time: 119 us -> 85.8 us (0.72)
  Pallas kernels: 101 us -> 63 us
  waiting for transfers between devices: 4.08 us -> 9.24 us
    pallas_call x7, Pallas kernels: 101 us -> 63 us  [call(): pl.pallas_call(kernel, name=name, out_shape=[jax.ShapeDtypeStruct(shape,...]
    ppermute x7 -> x6, waiting for transfers between devices: 4.08 us -> 9.24 us  [partner(): lax.ppermute(x, axis, [(i, i ^ 1 << bit) for i in range(lax.axis_size(axi...]
    ppermute x7 -> x6, starting transfers between devices: 7.44 us -> 6.93 us  [partner(): lax.ppermute(x, axis, [(i, i ^ 1 << bit) for i in range(lax.axis_size(axi...]
    unnamed x22 -> x20, local copies, waits for them, and re-layouts: 3.79 us -> 3.73 us
  transfers between devices with their start and end apart: 7 -> 6, of which waited for: 1 -> 1; matrix products, arithmetic and copies ran while one was open for 2% -> 0% of each run, Pallas kernels for 53% -> 36%
where the time goes in v1:
time: 85.8 us; the launch traced here: 85.5 us
  Pallas kernels  63 us (73%)
  waiting for transfers between devices  9.24 us (11%)
  starting transfers between devices  6.93 us (8%)
  local copies, waits for them, and re-layouts  3.78 us (4%)
  other arithmetic  1.78 us (2%)
    pallas_call x7, Pallas kernels, call(): pl.pallas_call(kernel, name=name, out_shape=[jax.ShapeDtypeStruct(shape,...  63 us
    ppermute x6, waiting for transfers between devices, partner(): lax.ppermute(x, axis, [(i, i ^ 1 << bit) for i in range(lax.axis_size(axi...  9.24 us
    ppermute x6, starting transfers between devices, partner(): lax.ppermute(x, axis, [(i, i ^ 1 << bit) for i in range(lax.axis_size(axi...  6.93 us
    unnamed x20, local copies, waits for them, and re-layouts  3.73 us
    another operation x1, other arithmetic, body(): return (reduced[0][None], jnp.stack(reduced[1:], axis=0), factor)  1.78 us
  transfers between devices with their start and end apart: 6, of which 1 were waited for; matrix products, arithmetic and copies ran while one was open for 0% of the time, Pallas kernels for 36%

profile of v1, /device:TPU:0, one launch (start us, length us, event | category | flops | bytes accessed | tf_op | source)
XLA Modules:
  0.0 85.5 jit_solution(14547345792042044291)
XLA Ops:
  0.6 0.0 copy-start.4
  0.7 16.5 %leaf.1.g_ref.x_ref = f32[256,256]{1,0:T(8,128)} custom-call(s32[3,32]{1,0:T(4,128)} %rank_ref.11, f32[512,512]{1,0:T(8,128)} %bitcast.12, f32[512,256]{1,0:T(8,128)} %bitcast.13), custom_call_target="tpu_custom_call" | custom-call | flops 8000000000 | bytes 4000000 | tf_op jit(solution)/shard_map/leaf/pallas_call | solution.py:348
  17.2 3.0 %collective-permute-start = (f32[256,256]{1,0:T(8,128)}, f32[256,256]{1,0:T(8,128)}, u32[]{:S(2)}, u32[]{:S(2)}) collective-permute-start(f32[256,256]{1,0:T(8,128)} %leaf.1.g_ref.x_ref), channel_id=1, source_target_pairs={{0,1},{1,0},{2,3},{3,2},{4,5},{5,4},{6,7},{7,6},{8,9},{9,8},{10,11... | collective-permute-start | bytes 786440 | tf_op jit(solution)/shard_map/ppermute | solution.py:360
  20.2 0.0 collective-permute-start.1
  20.2 0.0 copy-start.1
  20.2 2.1 %collective-permute-start.3 = (f32[2,256,256]{2,1,0:T(8,128)S(1)}, f32[2,256,256]{2,1,0:T(8,128)S(1)}, u32[]{:S(2)}, u32[]{:S(2)}) collective-permute-start(f32[2,256,256]{2,1,0:T(8,128)S(1)} %slice_bitcast_fusion.mine_ref), channel_id=1, source_target_pairs={{0,2},{1,3},{2,0},{3,1},{4,6},{5,7},{6,4},{7,5},{8,10},{9,11},{10,... | collective-permute-start | bytes 1572872 | tf_op jit(solution)/shard_map/ppermute | solution.py:360
  22.4 0.1 collective-permute-start.5
  22.5 6.2 %first.1.before_ref = f32[256,256]{1,0:T(8,128)} custom-call(f32[256,256]{1,0:T(8,128)} %leaf.1.g_ref.x_ref), custom_call_target="tpu_custom_call" | custom-call | flops 4000000000 | bytes 4000000 | tf_op jit(solution)/shard_map/first/pallas_call | solution.py:348
  28.7 0.0 collective-permute-done.y_ref
  28.7 9.2 %collective-permute-done.1.theirs_ref = f32[2,256,256]{2,1,0:T(8,128)S(1)} collective-permute-done((f32[2,256,256]{2,1,0:T(8,128)S(1)}, f32[2,256,256]{2,1,0:T(8,128)S(1)}, u32[]{:S(2)}, u32[]{:S(2)}) %collective-permute-start.1) | collective-permute-done | bytes 524320 | tf_op jit(solution)/shard_map/ppermute | solution.py:360
  37.9 0.8 copy-done.6
  38.7 5.4 %merge.2.g_ref.x_ref = f32[256,256]{1,0:T(8,128)} custom-call(s32[3,32]{1,0:T(4,128)} %rank_ref.11, f32[256,256]{1,0:T(8,128)} %leaf.1.g_ref.x_ref, f32[256,256]{1,0:T(8,128)} %collective-permute-done.y_ref, f32[2,256,256]{2,1,0:T(8,128)} %bitcast.14, f32[2,256,256]{2,1,0:T(8,128)} %copy-done.6), custom_call_target="tpu_custom_call" | custom-call | flops 1000000000 | bytes 4000000 | tf_op jit(solution)/shard_map/merge/pallas_call | solution.py:348
  44.1 1.8 %collective-permute-start.2 = (f32[256,256]{1,0:T(8,128)}, f32[256,256]{1,0:T(8,128)S(1)}, u32[]{:S(2)}, u32[]{:S(2)}) collective-permute-start(f32[256,256]{1,0:T(8,128)} %merge.2.g_ref.x_ref), channel_id=1, source_target_pairs={{0,2},{1,3},{2,0},{3,1},{4,6},{5,7},{6,4},{7,5},{8,10},{9,11},{10,... | collective-permute-start | bytes 786440 | tf_op jit(solution)/shard_map/ppermute | solution.py:360
  45.9 7.1 %middle.1 = (f32[256,256]{1,0:T(8,128)}, f32[256,256]{1,0:T(8,128)}) custom-call(s32[3,32]{1,0:T(4,128)} %rank_ref.11, f32[256,256]{1,0:T(8,128)} %first.1.before_ref, f32[256,256]{1,0:T(8,128)} %merge.2.g_ref.x_ref), custom_call_target="tpu_custom_call" | custom-call | flops 4000000000 | bytes 4000000 | tf_op jit(solution)/shard_map/middle/pallas_call | solution.py:348
  53.0 0.0 collective-permute-done.3.theirs_ref
  53.0 0.0 collective-permute-done.2.y_ref
  53.0 0.8 copy-done.5
  53.8 0.7 copy-done.8
  54.5 5.1 %merge.3.g_ref = f32[256,256]{1,0:T(8,128)} custom-call(s32[3,32]{1,0:T(4,128)} %rank_ref.11, f32[256,256]{1,0:T(8,128)} %merge.2.g_ref.x_ref, f32[256,256]{1,0:T(8,128)} %copy-done.8, f32[2,256,256]{2,1,0:T(8,128)} %copy-done.1, f32[2,256,256]{2,1,0:T(8,128)} %copy-done.5), custom_call_target="tpu_custom_call" | custom-call | flops 1000000000 | bytes 4000000 | tf_op jit(solution)/shard_map/merge/pallas_call | solution.py:348
  59.7 6.5 %final.1 = f32[256,256]{1,0:T(8,128)} custom-call(s32[3,32]{1,0:T(4,128)} %rank_ref.11, f32[256,256]{1,0:T(8,128)} %get-tuple-element.8.before_ref), custom_call_target="tpu_custom_call" | custom-call | flops 4000000000 | bytes 4000000 | tf_op jit(solution)/shard_map/final/pallas_call | solution.py:348
  66.1 0.7 copy-done.7
  66.8 0.7 copy-done.9
  67.5 16.1 %top.1 = (f32[512,512]{1,0:T(8,128)}, f32[256,256]{1,0:T(8,128)}) custom-call(s32[3,32]{1,0:T(4,128)} %rank_ref.11, f32[256,256]{1,0:T(8,128)} %merge.3.g_ref, f32[256,256]{1,0:T(8,128)} %copy-done.9, f32[256,256]{1,0:T(8,128)} %copy-done.2, f32[256,256]{1,0:T(8,128)} %copy-done.7), custom_call_target="tpu_custom_call" | custom-call | flops 4000000000 | bytes 4000000 | tf_op jit(solution)/shard_map/top/pallas_call | solution.py:348
  83.7 1.8 %pad_maximum_fusion = f32[2,256,256]{2,1,0:T(8,128)} fusion(f32[1,256,256]{2,1,0:T(8,128)} %bitcast.11, f32[1,256,256]{2,1,0:T(8,128)S(1)} %bitcast.10), kind=kLoop, calls=%fused_computation | loop fusion | flops 131072 | bytes 1048576 | tf_op jit(solution)/shard_map/stack | solution.py:391
  (18 shorter events, 0.1 us)
Async XLA Ops:
  0.6 19.5 %copy-start.4 = (f32[1,2,256,256]{3,2,1,0:T(8,128)S(1)}, f32[1,2,256,256]{3,2,1,0:T(8,128)}, u32[]{:S(2)}) copy-start(f32[1,2,256,256]{3,2,1,0:T(8,128)} %param.7) | copy-start | bytes 1572868
  0.6 19.6 %copy-start = (f32[2,2,256,256]{3,2,1,0:T(8,128)S(1)}, f32[2,2,256,256]{3,2,1,0:T(8,128)}, u32[]{:S(2)}) copy-start(f32[2,2,256,256]{3,2,1,0:T(8,128)} %param.8) | copy-start | bytes 3145732
  17.2 11.5 %collective-permute-start = (f32[256,256]{1,0:T(8,128)}, f32[256,256]{1,0:T(8,128)}, u32[]{:S(2)}, u32[]{:S(2)}) collective-permute-start(f32[256,256]{1,0:T(8,128)} %leaf.1.g_ref.x_ref), channel_id=1, source_target_pairs={{0,1},{1,0},{2,3},{3,2},{4,5},{5,4},{6,7},{7,6},{8,9},{9,8},{10,11... | collective-permute-start | bytes 786440 | tf_op jit(solution)/shard_map/ppermute | solution.py:360
  20.2 17.8 %collective-permute-start.1 = (f32[2,256,256]{2,1,0:T(8,128)S(1)}, f32[2,256,256]{2,1,0:T(8,128)S(1)}, u32[]{:S(2)}, u32[]{:S(2)}) collective-permute-start(f32[2,256,256]{2,1,0:T(8,128)S(1)} %bitcast.15), channel_id=1, source_target_pairs={{0,1},{1,0},{2,3},{3,2},{4,5},{5,4},{6,7},{7,6},{8,9},{9,8},{10,11... | collective-permute-start | bytes 1572872 | tf_op jit(solution)/shard_map/ppermute | solution.py:360
  20.2 8.5 %copy-start.1 = (f32[2,256,256]{2,1,0:T(8,128)}, f32[2,256,256]{2,1,0:T(8,128)S(1)}, u32[]{:S(2)}) copy-start(f32[2,256,256]{2,1,0:T(8,128)S(1)} %slice_bitcast_fusion.mine_ref) | copy-start | bytes 1572868
  20.2 32.8 %collective-permute-start.3 = (f32[2,256,256]{2,1,0:T(8,128)S(1)}, f32[2,256,256]{2,1,0:T(8,128)S(1)}, u32[]{:S(2)}, u32[]{:S(2)}) collective-permute-start(f32[2,256,256]{2,1,0:T(8,128)S(1)} %slice_bitcast_fusion.mine_ref), channel_id=1, source_target_pairs={{0,2},{1,3},{2,0},{3,1},{4,6},{5,7},{6,4},{7,5},{8,10},{9,11},{10,... | collective-permute-start | bytes 1572872 | tf_op jit(solution)/shard_map/ppermute | solution.py:360
  22.4 6.3 %copy-start.2 = (f32[256,256]{1,0:T(8,128)}, f32[256,256]{1,0:T(8,128)S(1)}, u32[]{:S(2)}) copy-start(f32[256,256]{1,0:T(8,128)S(1)} %slice_bitcast_fusion.1.c_ref) | copy-start | bytes 786436
  22.4 43.7 %collective-permute-start.5 = (f32[256,256]{1,0:T(8,128)S(1)}, f32[256,256]{1,0:T(8,128)S(1)}, u32[]{:S(2)}, u32[]{:S(2)}) collective-permute-start(f32[256,256]{1,0:T(8,128)S(1)} %slice_bitcast_fusion.1.c_ref), channel_id=1, source_target_pairs={{0,4},{4,0},{8,12},{12,8},{16,20},{20,16},{24,28},{28,24},{1,5},{5... | collective-permute-start | bytes 786440 | tf_op jit(solution)/shard_map/ppermute | solution.py:360
  37.9 0.8 copy-start.6
  44.1 8.9 %collective-permute-start.2 = (f32[256,256]{1,0:T(8,128)}, f32[256,256]{1,0:T(8,128)S(1)}, u32[]{:S(2)}, u32[]{:S(2)}) collective-permute-start(f32[256,256]{1,0:T(8,128)} %merge.2.g_ref.x_ref), channel_id=1, source_target_pairs={{0,2},{1,3},{2,0},{3,1},{4,6},{5,7},{6,4},{7,5},{8,10},{9,11},{10,... | collective-permute-start | bytes 786440 | tf_op jit(solution)/shard_map/ppermute | solution.py:360
  53.0 0.8 copy-start.5
  53.8 0.7 copy-start.8
  59.7 6.5 %collective-permute-start.4 = (f32[256,256]{1,0:T(8,128)}, f32[256,256]{1,0:T(8,128)S(1)}, u32[]{:S(2)}, u32[]{:S(2)}) collective-permute-start(f32[256,256]{1,0:T(8,128)} %merge.3.g_ref), channel_id=1, source_target_pairs={{0,4},{4,0},{8,12},{12,8},{16,20},{20,16},{24,28},{28,24},{1,5},{5... | collective-permute-start | bytes 786440 | tf_op jit(solution)/shard_map/ppermute | solution.py:360
  66.1 17.6 %copy-start.3 = (f32[256,256]{1,0:T(8,128)S(1)}, f32[256,256]{1,0:T(8,128)}, u32[]{:S(2)}) copy-start(f32[256,256]{1,0:T(8,128)} %final.1) | copy-start | bytes 786436
  66.1 0.7 copy-start.7
  66.8 0.7 copy-start.9

commit v2 on v1

--- a/solution.py
+++ b/solution.py
@@ -12,6 +12,7 @@
 PANEL = 32
 TOLERANCE = 4e-6
 MOST = 40
+GRANT = 20 * 2**20
 HIGH = lax.Precision.HIGHEST
 
 
@@ -20,7 +21,6 @@
 
 
 NT = ((1,), (1,))
-TN = ((0,), (0,))
 
 
 def thirds(x):
@@ -315,8 +315,11 @@
     return upper.T
 
 
-def top_kernel(depth, rank_ref, g_ref, go_ref, c_ref, co_ref, f_ref, l_ref, a_ref, b_ref, ka_ref, kb_ref, s_ref, *work):
+def top_kernel(depth, rank_ref, g_ref, go_ref, c_ref, co_ref, *refs):
     n = g_ref.shape[0]
+    lower, (f_ref, out_ref, l_ref, a_ref, b_ref, ka_ref, kb_ref, s_ref), work = refs[: depth - 1], refs[depth - 1 : depth + 7], refs[depth + 7 :]
+    for i, ref in enumerate(lower):
+        out_ref[i] = ref[...]
     pos = lax.axis_index("outer")
     first = jnp.bitwise_and(pos, 1) == 0
     node = jnp.bitwise_and(pos, -2)
@@ -335,23 +338,23 @@
     eliminate([a_ref, b_ref], [ka_ref, kb_ref], reverse=True)
     e = ka_ref[...]
     rank = jnp.where(first, ra, rb)
-    l_ref[...] = both(n, rank, rank, jnp.where(pick, a_ref[...], b_ref[...] + l_ref[...]))
+    out_ref[depth - 1] = both(n, rank, rank, jnp.where(pick, a_ref[...], b_ref[...] + l_ref[...]))
     f_ref[:n, :n] = factor_of(n, e)
     f_ref[:n, n:] = jnp.zeros((n, n), jnp.float32)
     f_ref[n:, :n] = dot6(thirds(s_ref[...]), thirds(jnp.where(row >= col, e, 0.0)), nt=True)
     f_ref[n:, n:] = factor_of(n, kb_ref[...])
 
 
-def call(kernel, name, outs, n, scratch, *arrays, ranks=None, flops=10**9):
+def call(kernel, outs, n, scratch, *arrays, ranks=None, flops=10**9):
     vmem = pl.BlockSpec(memory_space=pltpu.VMEM)
     lead = [] if ranks is None else [pl.BlockSpec(memory_space=pltpu.SMEM)]
     return pl.pallas_call(
         kernel,
-        name=name,
         out_shape=[jax.ShapeDtypeStruct(shape, jnp.float32) for shape in outs],
         in_specs=lead + [vmem] * len(arrays),
         out_specs=[vmem] * len(outs),
         scratch_shapes=[pltpu.VMEM((n, n), jnp.float32)] * scratch,
+        compiler_params=pltpu.CompilerParams(vmem_limit_bytes=GRANT),
         cost_estimate=pl.CostEstimate(flops=flops, bytes_accessed=4 * 10**6, transcendentals=0),
     )(*([] if ranks is None else [ranks]), *arrays)
 
@@ -360,40 +363,42 @@
     return lax.ppermute(x, axis, [(i, i ^ 1 << bit) for i in range(lax.axis_size(axis))])
 
 
-def body(leaf_blocks, leaf_bases, local_gens, chain_gens, node_ranks):
+def steps(leaf_blocks, leaf_bases, local_gens, chain_gens, node_ranks):
     n = leaf_bases.shape[2]
     in_levels = chain_gens.shape[0]
     square = (n, n)
     gens = [local_gens[0]] + [chain_gens[d] for d in range(in_levels)]
-    others = [partner(gens[d], "inner", d) for d in range(in_levels)]
+    others = []
+    for d in range(in_levels):
+        others.append(partner(gens[d], "inner", d))
     couple = gens[in_levels][1]
     other_couple = partner(couple, "outer", 0)
-    g = call(leaf_kernel, "leaf", [square], n, 7, leaf_blocks[0], leaf_bases[0], ranks=node_ranks, flops=8 * 10**9)[0]
+    g = call(leaf_kernel, [square], n, 7, leaf_blocks[0], leaf_bases[0], ranks=node_ranks, flops=8 * 10**9)[0]
     reduced = []
     half = None
     for depth in range(in_levels):
         g_other = partner(g, "inner", depth)
         if depth == 0:
-            half = call(first_kernel, "first", [square], n, 0, g, flops=4 * 10**9)[0]
+            half = call(first_kernel, [square], n, 0, g, flops=4 * 10**9)[0]
         else:
             middle = functools.partial(middle_kernel, depth)
-            done, half = call(middle, "middle", [square] * 2, n, 1, half, g, ranks=node_ranks, flops=4 * 10**9)
+            done, half = call(middle, [square] * 2, n, 1, half, g, ranks=node_ranks, flops=4 * 10**9)
             reduced.append(done)
         merge = functools.partial(merge_kernel, depth)
-        g = call(merge, "merge", [square], n, 5, g, g_other, gens[depth], others[depth], ranks=node_ranks)[0]
+        g = call(merge, [square], n, 5, g, g_other, gens[depth], others[depth], ranks=node_ranks)[0]
     g_other = partner(g, "outer", 0)
     final = functools.partial(final_kernel, in_levels)
-    reduced.append(call(final, "final", [square], n, 1, half, ranks=node_ranks, flops=4 * 10**9)[0])
+    reduced.append(call(final, [square], n, 1, half, ranks=node_ranks, flops=4 * 10**9)[0])
     top = functools.partial(top_kernel, in_levels)
-    arrays = (g, g_other, couple, other_couple)
-    factor, done = call(top, "top", [(2 * n, 2 * n), square], n, 9, *arrays, ranks=node_ranks, flops=4 * 10**9)
-    reduced.append(done)
-    return (reduced[0][None], jnp.stack(reduced[1:], axis=0), factor)
+    arrays = (g, g_other, couple, other_couple, *reduced[1:])
+    outs = [(2 * n, 2 * n), (in_levels, n, n)]
+    factor, chain = call(top, outs, n, 10, *arrays, ranks=node_ranks, flops=4 * 10**9)
+    return (reduced[0][None], chain, factor)
 
 
 def solution(mesh):
     return jax.shard_map(
-        body,
+        steps,
         mesh=mesh,
         in_specs=(
             P(("outer", "inner"), None, None),

time: 85.8 us -> 76.4 us (0.89)
  Pallas kernels: 63 us -> 54.6 us
  other arithmetic: 1.78 us -> 0 us
  waiting for transfers between devices: 9.24 us -> 10.9 us
  local copies, waits for them, and re-layouts: 3.78 us -> 2.43 us
    pallas_call x7, Pallas kernels: 63 us -> 54.6 us  [call(): pl.pallas_call(kernel, out_shape=[jax.ShapeDtypeStruct(shape, jnp.float32...]
    unnamed x20 -> x10, local copies, waits for them, and re-layouts: 3.73 us -> 1.37 us
    another operation x1 -> x0, other arithmetic: 1.78 us -> none  [body(): return (reduced[0][None], jnp.stack(reduced[1:], axis=0), factor)]
    ppermute x6, waiting for transfers between devices: 9.24 us -> 10.9 us  [partner(): lax.ppermute(x, axis, [(i, i ^ 1 << bit) for i in range(lax.axis_size(axi...]
    squeeze x2, local copies, waits for them, and re-layouts: 0.05 us -> 1.06 us  [the longest x1 1.03 us: steps(): couple = gens[in_levels][1]]
  transfers between devices with their start and end apart: 6 -> 6, of which waited for: 1 -> 2; matrix products, arithmetic and copies ran while one was open for 0% -> 0% of each run, Pallas kernels for 36% -> 51%
where the time goes in v2:
time: 76.4 us; the launch traced here: 76.2 us
  Pallas kernels  54.6 us (71%)
  waiting for transfers between devices  10.9 us (14%)
  starting transfers between devices  7.61 us (10%)
  local copies, waits for them, and re-layouts  2.43 us (3%)
    pallas_call x7, Pallas kernels, call(): pl.pallas_call(kernel, out_shape=[jax.ShapeDtypeStruct(shape, jnp.float32...  54.6 us
    ppermute x6, waiting for transfers between devices, partner(): lax.ppermute(x, axis, [(i, i ^ 1 << bit) for i in range(lax.axis_size(axi...  10.9 us
    ppermute x6, starting transfers between devices, partner(): lax.ppermute(x, axis, [(i, i ^ 1 << bit) for i in range(lax.axis_size(axi...  7.61 us
  transfers between devices with their start and end apart: 6, of which 2 were waited for; matrix products, arithmetic and copies ran while one was open for 0% of the time, Pallas kernels for 51%

profile of v2, /device:TPU:0, one launch (start us, length us, event | category | flops | bytes accessed | tf_op | source)
XLA Modules:
  0.0 76.2 jit_solution(555611416655394441)
XLA Ops:
  0.6 1.0 %slice_bitcast_fusion.1.c_ref = f32[256,256]{1,0:T(8,128)S(1)} fusion(f32[2,2,256,256]{3,2,1,0:T(8,128)} %param.8), kind=kLoop, calls=%fused_computation.1 | loop fusion | bytes 524288 | tf_op jit(solution)/shard_map/squeeze | solution.py:374
  1.7 0.0 copy-start.3
  1.7 0.6 collective-permute-start.5
  2.2 0.0 copy-done.1
  2.2 0.1 copy-done.3
  2.4 1.2 %copy-done = f32[1,512,512]{2,1,0:T(8,128)S(1)} copy-done((f32[1,512,512]{2,1,0:T(8,128)S(1)}, f32[1,512,512]{2,1,0:T(8,128)}, u32[]{:S(2)}) %copy-start) | copy-done | bytes 1048600
  3.6 15.0 %shard_map.76.g_ref.x_ref = f32[256,256]{1,0:T(8,128)S(1)} custom-call(s32[3,32]{1,0:T(4,128)S(1)} %copy-done.3, f32[512,512]{1,0:T(8,128)S(1)} %bitcast.8, f32[512,256]{1,0:T(8,128)S(1)} %bitcast.9), custom_call_target="tpu_custom_call" | custom-call | flops 8000000000 | bytes 4000000 | tf_op jit(solution)/shard_map/pallas_call | solution.py:351
  18.6 3.0 %collective-permute-start = (f32[256,256]{1,0:T(8,128)S(1)}, f32[256,256]{1,0:T(8,128)S(1)}, u32[]{:S(2)}, u32[]{:S(2)}) collective-permute-start(f32[256,256]{1,0:T(8,128)S(1)} %shard_map.76.g_ref.x_ref), channel_id=1, source_target_pairs={{0,1},{1,0},{2,3},{3,2},{4,5},{5,4},{6,7},{7,6},{8,9},{9,8},{10,11... | collective-permute-start | bytes 786440 | tf_op jit(solution)/shard_map/ppermute | solution.py:363
  21.6 0.1 collective-permute-start.1
  21.7 2.0 %collective-permute-start.3 = (f32[2,256,256]{2,1,0:T(8,128)S(1)}, f32[2,256,256]{2,1,0:T(8,128)S(1)}, u32[]{:S(2)}, u32[]{:S(2)}) collective-permute-start(f32[2,256,256]{2,1,0:T(8,128)S(1)} %slice_bitcast_fusion.mine_ref), channel_id=1, source_target_pairs={{0,2},{1,3},{2,0},{3,1},{4,6},{5,7},{6,4},{7,5},{8,10},{9,11},{10,... | collective-permute-start | bytes 1572872 | tf_op jit(solution)/shard_map/ppermute | solution.py:363
  23.8 4.6 %shard_map.77.before_ref = f32[256,256]{1,0:T(8,128)S(1)} custom-call(f32[256,256]{1,0:T(8,128)S(1)} %shard_map.76.g_ref.x_ref), custom_call_target="tpu_custom_call" | custom-call | flops 4000000000 | bytes 4000000 | tf_op jit(solution)/shard_map/pallas_call | solution.py:351
  28.4 0.4 collective-permute-done.y_ref
  28.8 10.4 %collective-permute-done.1.theirs_ref = f32[2,256,256]{2,1,0:T(8,128)S(1)} collective-permute-done((f32[2,256,256]{2,1,0:T(8,128)S(1)}, f32[2,256,256]{2,1,0:T(8,128)S(1)}, u32[]{:S(2)}, u32[]{:S(2)}) %collective-permute-start.1) | collective-permute-done | bytes 524320 | tf_op jit(solution)/shard_map/ppermute | solution.py:363
  39.2 3.9 %shard_map.78.g_ref.x_ref = f32[256,256]{1,0:T(8,128)S(1)} custom-call(s32[3,32]{1,0:T(4,128)S(1)} %copy-done.3, f32[256,256]{1,0:T(8,128)S(1)} %shard_map.76.g_ref.x_ref, f32[256,256]{1,0:T(8,128)S(1)} %collective-permute-done.y_ref, f32[2,256,256]{2,1,0:T(8,128)S(1)} %bitcast.11, f32[2,256,256]{2,1,0:T(8,128)S(1)} %collective-permute-done.1.theirs_ref), custom_call_target="tpu_custom_call" | custom-call | flops 1000000000 | bytes 4000000 | tf_op jit(solution)/shard_map/pallas_call | solution.py:351
  43.1 1.8 %collective-permute-start.2 = (f32[256,256]{1,0:T(8,128)S(1)}, f32[256,256]{1,0:T(8,128)S(1)}, u32[]{:S(2)}, u32[]{:S(2)}) collective-permute-start(f32[256,256]{1,0:T(8,128)S(1)} %shard_map.78.g_ref.x_ref), channel_id=1, source_target_pairs={{0,2},{1,3},{2,0},{3,1},{4,6},{5,7},{6,4},{7,5},{8,10},{9,11},{10,... | collective-permute-start | bytes 786440 | tf_op jit(solution)/shard_map/ppermute | solution.py:363
  44.9 6.5 %shard_map.79 = (f32[256,256]{1,0:T(8,128)}, f32[256,256]{1,0:T(8,128)S(1)}) custom-call(s32[3,32]{1,0:T(4,128)S(1)} %copy-done.3, f32[256,256]{1,0:T(8,128)S(1)} %shard_map.77.before_ref, f32[256,256]{1,0:T(8,128)S(1)} %shard_map.78.g_ref.x_ref), custom_call_target="tpu_custom_call" | custom-call | flops 4000000000 | bytes 4000000 | tf_op jit(solution)/shard_map/pallas_call | solution.py:351
  51.4 0.0 collective-permute-done.3.theirs_ref
  51.4 0.0 collective-permute-done.2.y_ref
  51.4 3.7 %shard_map.80.g_ref = f32[256,256]{1,0:T(8,128)S(1)} custom-call(s32[3,32]{1,0:T(4,128)S(1)} %copy-done.3, f32[256,256]{1,0:T(8,128)S(1)} %shard_map.78.g_ref.x_ref, f32[256,256]{1,0:T(8,128)S(1)} %collective-permute-done.2.y_ref, f32[2,256,256]{2,1,0:T(8,128)S(1)} %slice_bitcast_fusion.mine_ref, f32[2,256,256]{2,1,0:T(8,128)S(1)} %collective-permute-done.3.theirs_ref), custom_call_target="tpu_custom_call" | custom-call | flops 1000000000 | bytes 4000000 | tf_op jit(solution)/shard_map/pallas_call | solution.py:351
  55.1 0.1 collective-permute-start.4
  55.2 5.3 %shard_map.81.refs_0_ = f32[256,256]{1,0:T(8,128)S(1)} custom-call(s32[3,32]{1,0:T(4,128)S(1)} %copy-done.3, f32[256,256]{1,0:T(8,128)S(1)} %get-tuple-element.8.before_ref), custom_call_target="tpu_custom_call" | custom-call | flops 4000000000 | bytes 4000000 | tf_op jit(solution)/shard_map/pallas_call | solution.py:351
  60.5 0.0 collective-permute-done.5.co_ref
  60.5 0.0 collective-permute-done.4.go_ref
  60.5 15.6 %shard_map.82 = (f32[512,512]{1,0:T(8,128)}, f32[2,256,256]{2,1,0:T(8,128)}) custom-call(s32[3,32]{1,0:T(4,128)S(1)} %copy-done.3, f32[256,256]{1,0:T(8,128)S(1)} %shard_map.80.g_ref, f32[256,256]{1,0:T(8,128)S(1)} %collective-permute-done.4.go_ref, f32[256,256]{1,0:T(8,128)S(1)} %slice_bitcast_fusion.1.c_ref, f32[256,256]{1,0:T(8,128)S(1)} %collective-permute-done.5.co_ref, ...), custom_call_target="tpu_custom_call" | custom-call | flops 4000000000 | bytes 4000000 | tf_op jit(solution)/shard_map/pallas_call | solution.py:351
  (7 shorter events, 0.0 us)
Async XLA Ops:
  0.6 1.6 %copy-start.1 = (f32[1,512,256]{2,1,0:T(8,128)S(1)}, f32[1,512,256]{2,1,0:T(8,128)}, u32[]{:S(2)}) copy-start(f32[1,512,256]{2,1,0:T(8,128)} %param.6) | copy-start | bytes 1572868
  1.7 0.7 copy-start.3
  1.7 58.8 %collective-permute-start.5 = (f32[256,256]{1,0:T(8,128)S(1)}, f32[256,256]{1,0:T(8,128)S(1)}, u32[]{:S(2)}, u32[]{:S(2)}) collective-permute-start(f32[256,256]{1,0:T(8,128)S(1)} %slice_bitcast_fusion.1.c_ref), channel_id=1, source_target_pairs={{0,4},{4,0},{8,12},{12,8},{16,20},{20,16},{24,28},{28,24},{1,5},{5... | collective-permute-start | bytes 786440 | tf_op jit(solution)/shard_map/ppermute | solution.py:363
  2.4 1.2 %copy-start = (f32[1,512,512]{2,1,0:T(8,128)S(1)}, f32[1,512,512]{2,1,0:T(8,128)}, u32[]{:S(2)}) copy-start(f32[1,512,512]{2,1,0:T(8,128)} %param.5) | copy-start | bytes 3145732
  3.6 18.0 %copy-start.2 = (f32[1,2,256,256]{3,2,1,0:T(8,128)S(1)}, f32[1,2,256,256]{3,2,1,0:T(8,128)}, u32[]{:S(2)}) copy-start(f32[1,2,256,256]{3,2,1,0:T(8,128)} %param.7) | copy-start | bytes 1572868
  3.6 18.1 %copy-start.4 = (f32[2,2,256,256]{3,2,1,0:T(8,128)S(1)}, f32[2,2,256,256]{3,2,1,0:T(8,128)}, u32[]{:S(2)}) copy-start(f32[2,2,256,256]{3,2,1,0:T(8,128)} %param.8) | copy-start | bytes 3145732
  18.6 10.2 %collective-permute-start = (f32[256,256]{1,0:T(8,128)S(1)}, f32[256,256]{1,0:T(8,128)S(1)}, u32[]{:S(2)}, u32[]{:S(2)}) collective-permute-start(f32[256,256]{1,0:T(8,128)S(1)} %shard_map.76.g_ref.x_ref), channel_id=1, source_target_pairs={{0,1},{1,0},{2,3},{3,2},{4,5},{5,4},{6,7},{7,6},{8,9},{9,8},{10,11... | collective-permute-start | bytes 786440 | tf_op jit(solution)/shard_map/ppermute | solution.py:363
  21.6 17.6 %collective-permute-start.1 = (f32[2,256,256]{2,1,0:T(8,128)S(1)}, f32[2,256,256]{2,1,0:T(8,128)S(1)}, u32[]{:S(2)}, u32[]{:S(2)}) collective-permute-start(f32[2,256,256]{2,1,0:T(8,128)S(1)} %bitcast.10), channel_id=1, source_target_pairs={{0,1},{1,0},{2,3},{3,2},{4,5},{5,4},{6,7},{7,6},{8,9},{9,8},{10,11... | collective-permute-start | bytes 1572872 | tf_op jit(solution)/shard_map/ppermute | solution.py:363
  21.7 29.7 %collective-permute-start.3 = (f32[2,256,256]{2,1,0:T(8,128)S(1)}, f32[2,256,256]{2,1,0:T(8,128)S(1)}, u32[]{:S(2)}, u32[]{:S(2)}) collective-permute-start(f32[2,256,256]{2,1,0:T(8,128)S(1)} %slice_bitcast_fusion.mine_ref), channel_id=1, source_target_pairs={{0,2},{1,3},{2,0},{3,1},{4,6},{5,7},{6,4},{7,5},{8,10},{9,11},{10,... | collective-permute-start | bytes 1572872 | tf_op jit(solution)/shard_map/ppermute | solution.py:363
  43.1 8.4 %collective-permute-start.2 = (f32[256,256]{1,0:T(8,128)S(1)}, f32[256,256]{1,0:T(8,128)S(1)}, u32[]{:S(2)}, u32[]{:S(2)}) collective-permute-start(f32[256,256]{1,0:T(8,128)S(1)} %shard_map.78.g_ref.x_ref), channel_id=1, source_target_pairs={{0,2},{1,3},{2,0},{3,1},{4,6},{5,7},{6,4},{7,5},{8,10},{9,11},{10,... | collective-permute-start | bytes 786440 | tf_op jit(solution)/shard_map/ppermute | solution.py:363
  55.1 5.4 %collective-permute-start.4 = (f32[256,256]{1,0:T(8,128)S(1)}, f32[256,256]{1,0:T(8,128)S(1)}, u32[]{:S(2)}, u32[]{:S(2)}) collective-permute-start(f32[256,256]{1,0:T(8,128)S(1)} %shard_map.80.g_ref), channel_id=1, source_target_pairs={{0,4},{4,0},{8,12},{12,8},{16,20},{20,16},{24,28},{28,24},{1,5},{5... | collective-permute-start | bytes 786440 | tf_op jit(solution)/shard_map/ppermute | solution.py:363

commit v3 on v2

--- a/solution.py
+++ b/solution.py
@@ -287,24 +287,22 @@
     g_ref[...] = combine(2, x_ref, y_ref, s_ref, px, py, g_ref, work) + unit_rest(n, rp)
 
 
+def half_pass(a_ref, keep_ref, reverse, second):
+    tiles = a_ref.shape[0] // LANES
+    for i in range(tiles // 2, tiles) if second else range(tiles // 2):
+        yield from tile_pass(a_ref, keep_ref, reverse, tiles - 1 - i if reverse else i)
+
+
 def first_kernel(g_ref, half_ref):
     half_ref[...] = g_ref[...]
-    together([tile_pass(half_ref, None, False, 0)])
+    together([half_pass(half_ref, None, False, False)])
 
 
 def middle_kernel(depth, rank_ref, before_ref, g_ref, l_ref, half_ref, a_ref):
     n = g_ref.shape[0]
     a_ref[...] = before_ref[...]
     half_ref[...] = g_ref[...]
-    together([tile_pass(a_ref, None, False, 1), tile_pass(half_ref, None, False, 0)])
-    rank = rank_at(rank_ref, depth - 1)
-    l_ref[...] = both(n, rank, rank, a_ref[...])
-
-
-def final_kernel(depth, rank_ref, before_ref, l_ref, a_ref):
-    n = l_ref.shape[0]
-    a_ref[...] = before_ref[...]
-    together([tile_pass(a_ref, None, False, 1)])
+    together([half_pass(a_ref, None, False, True), half_pass(half_ref, None, False, False)])
     rank = rank_at(rank_ref, depth - 1)
     l_ref[...] = both(n, rank, rank, a_ref[...])
 
@@ -315,34 +313,50 @@
     return upper.T
 
 
-def top_kernel(depth, rank_ref, g_ref, go_ref, c_ref, co_ref, *refs):
-    n = g_ref.shape[0]
-    lower, (f_ref, out_ref, l_ref, a_ref, b_ref, ka_ref, kb_ref, s_ref), work = refs[: depth - 1], refs[depth - 1 : depth + 7], refs[depth + 7 :]
-    for i, ref in enumerate(lower):
-        out_ref[i] = ref[...]
+def group_pair(n, depth, rank_ref):
     pos = lax.axis_index("outer")
     first = jnp.bitwise_and(pos, 1) == 0
     node = jnp.bitwise_and(pos, -2)
-    ra, rb = rank_ref[depth, node], rank_ref[depth, node + 1]
-    row, col = iota((n, n), 0), iota((n, n), 1)
     pick = jnp.where(first, 1, 0) + jnp.zeros((n, n), jnp.int32) > 0
+    return first, pick, rank_ref[depth, node], rank_ref[depth, node + 1]
+
+
+def roots_kernel(depth, rank_ref, g_ref, go_ref, c_ref, co_ref, before_ref, *refs):
+    n = g_ref.shape[0]
+    lower = refs[: depth - 2]
+    keep_ref, s_ref, out_ref, l_ref, a_ref, b_ref, h_ref = refs[depth - 2 : depth + 5]
+    work = refs[depth + 5 :]
+    for i, ref in enumerate(lower):
+        out_ref[i] = ref[...]
+    first, pick, ra, rb = group_pair(n, depth, rank_ref)
     a_ref[...] = jnp.where(pick, g_ref[...], go_ref[...])
     b_ref[...] = jnp.where(pick, go_ref[...], g_ref[...])
     ca = jnp.where(pick, c_ref[...], co_ref[...])
     cb = jnp.where(pick, co_ref[...], c_ref[...])
     s_ref[...] = both(n, rb, ra, ca.T + cb)
+    h_ref[...] = before_ref[...]
     neumann(2, b_ref, a_ref, s_ref, b_ref[...], l_ref, work)
-    b_ref[...] = work[0][...]
-    back = dot6(thirds(dot6(thirds(s_ref[...]), thirds(a_ref[...]))), thirds(s_ref[...]), nt=True)
-    l_ref[...] = back
-    eliminate([a_ref, b_ref], [ka_ref, kb_ref], reverse=True)
-    e = ka_ref[...]
+    turned = thirds(s_ref[...])
+    back = dot6(thirds(dot6(turned, thirds(a_ref[...]))), turned, nt=True)
+    l_ref[...] = jnp.where(pick, 0.0, back)
+    a_ref[...] = jnp.where(pick, a_ref[...], work[0][...])
+    together([half_pass(a_ref, keep_ref, True, False), half_pass(h_ref, None, False, True)])
+    together([half_pass(a_ref, keep_ref, True, True)])
+    rank = rank_at(rank_ref, depth - 1)
+    out_ref[depth - 2] = both(n, rank, rank, h_ref[...])
     rank = jnp.where(first, ra, rb)
-    out_ref[depth - 1] = both(n, rank, rank, jnp.where(pick, a_ref[...], b_ref[...] + l_ref[...]))
+    out_ref[depth - 1] = both(n, rank, rank, a_ref[...] + l_ref[...])
+
+
+def top_kernel(depth, rank_ref, k_ref, ko_ref, s_ref, f_ref):
+    n = k_ref.shape[0]
+    _, pick, _, _ = group_pair(n, depth, rank_ref)
+    row, col = iota((n, n), 0), iota((n, n), 1)
+    e = jnp.where(pick, k_ref[...], ko_ref[...])
     f_ref[:n, :n] = factor_of(n, e)
     f_ref[:n, n:] = jnp.zeros((n, n), jnp.float32)
     f_ref[n:, :n] = dot6(thirds(s_ref[...]), thirds(jnp.where(row >= col, e, 0.0)), nt=True)
-    f_ref[n:, n:] = factor_of(n, kb_ref[...])
+    f_ref[n:, n:] = factor_of(n, jnp.where(pick, ko_ref[...], k_ref[...]))
 
 
 def call(kernel, outs, n, scratch, *arrays, ranks=None, flops=10**9):
@@ -367,32 +381,36 @@
     n = leaf_bases.shape[2]
     in_levels = chain_gens.shape[0]
     square = (n, n)
-    gens = [local_gens[0]] + [chain_gens[d] for d in range(in_levels)]
-    others = []
-    for d in range(in_levels):
+    gens = [local_gens[0]]
+    others = [partner(gens[0], "inner", 0)]
+    g = call(leaf_kernel, [square], n, 7, leaf_blocks[0], leaf_bases[0], ranks=node_ranks, flops=8 * 10**9)[0]
+    g_other = partner(g, "inner", 0)
+    g, chain_gens = lax.optimization_barrier((g, chain_gens))
+    gens = gens + [chain_gens[d] for d in range(in_levels)]
+    couple = gens[in_levels][1]
+    for d in range(1, in_levels):
         others.append(partner(gens[d], "inner", d))
-    couple = gens[in_levels][1]
     other_couple = partner(couple, "outer", 0)
-    g = call(leaf_kernel, [square], n, 7, leaf_blocks[0], leaf_bases[0], ranks=node_ranks, flops=8 * 10**9)[0]
     reduced = []
     half = None
     for depth in range(in_levels):
-        g_other = partner(g, "inner", depth)
         if depth == 0:
             half = call(first_kernel, [square], n, 0, g, flops=4 * 10**9)[0]
         else:
+            g_other = partner(g, "inner", depth)
             middle = functools.partial(middle_kernel, depth)
             done, half = call(middle, [square] * 2, n, 1, half, g, ranks=node_ranks, flops=4 * 10**9)
             reduced.append(done)
         merge = functools.partial(merge_kernel, depth)
         g = call(merge, [square], n, 5, g, g_other, gens[depth], others[depth], ranks=node_ranks)[0]
     g_other = partner(g, "outer", 0)
-    final = functools.partial(final_kernel, in_levels)
-    reduced.append(call(final, [square], n, 1, half, ranks=node_ranks, flops=4 * 10**9)[0])
+    roots = functools.partial(roots_kernel, in_levels)
+    arrays = (g, g_other, couple, other_couple, half, *reduced[1:])
+    outs = [square, square, (in_levels, n, n)]
+    e, s, chain = call(roots, outs, n, 8, *arrays, ranks=node_ranks, flops=4 * 10**9)
+    e_other = partner(e, "outer", 0)
     top = functools.partial(top_kernel, in_levels)
-    arrays = (g, g_other, couple, other_couple, *reduced[1:])
-    outs = [(2 * n, 2 * n), (in_levels, n, n)]
-    factor, chain = call(top, outs, n, 10, *arrays, ranks=node_ranks, flops=4 * 10**9)
+    factor = call(top, [(2 * n, 2 * n)], n, 0, e, e_other, s, ranks=node_ranks, flops=4 * 10**9)[0]
     return (reduced[0][None], chain, factor)
 
 

time: 76.4 us -> 67.6 us (0.88)
  Pallas kernels: 54.6 us -> 48.3 us
  waiting for transfers between devices: 10.9 us -> 8.54 us
    pallas_call x7, Pallas kernels: 54.6 us -> 48.3 us  [call(): pl.pallas_call(kernel, out_shape=[jax.ShapeDtypeStruct(shape, jnp.float32...]
    ppermute x6 -> x7, waiting for transfers between devices: 10.9 us -> 8.54 us  [partner(): lax.ppermute(x, axis, [(i, i ^ 1 << bit) for i in range(lax.axis_size(axi...]
    squeeze x1, local copies, waits for them, and re-layouts: 1.03 us -> 0.02 us  [steps(): couple = gens[in_levels][1]]
    unnamed x10, local copies, waits for them, and re-layouts: 1.37 us -> 2.28 us
    ppermute x6 -> x7, starting transfers between devices: 7.61 us -> 7.51 us  [partner(): lax.ppermute(x, axis, [(i, i ^ 1 << bit) for i in range(lax.axis_size(axi...]
  transfers between devices with their start and end apart: 6 -> 7, of which waited for: 2 -> 3; matrix products, arithmetic and copies ran while one was open for 0% -> 0% of each run, Pallas kernels for 51% -> 50%
where the time goes in v3:
time: 67.6 us; the launch traced here: 67.4 us
  Pallas kernels  48.3 us (71%)
  waiting for transfers between devices  8.54 us (13%)
  starting transfers between devices  7.51 us (11%)
  local copies, waits for them, and re-layouts  2.33 us (3%)
  between operations  0.71 us (1%)
    pallas_call x7, Pallas kernels, call(): pl.pallas_call(kernel, out_shape=[jax.ShapeDtypeStruct(shape, jnp.float32...  48.3 us
    ppermute x7, waiting for transfers between devices, partner(): lax.ppermute(x, axis, [(i, i ^ 1 << bit) for i in range(lax.axis_size(axi...  8.54 us
    ppermute x7, starting transfers between devices, partner(): lax.ppermute(x, axis, [(i, i ^ 1 << bit) for i in range(lax.axis_size(axi...  7.51 us
    unnamed x10, local copies, waits for them, and re-layouts  2.28 us
  transfers between devices with their start and end apart: 7, of which 3 were waited for; matrix products, arithmetic and copies ran while one was open for 0% of the time, Pallas kernels for 50%

profile of v3, /device:TPU:0, one launch (start us, length us, event | category | flops | bytes accessed | tf_op | source)
XLA Modules:
  0.0 67.4 jit_solution(337100527188042135)
XLA Ops:
  0.6 3.0 %collective-permute-start.1 = (f32[2,256,256]{2,1,0:T(8,128)}, f32[2,256,256]{2,1,0:T(8,128)S(1)}, u32[]{:S(2)}, u32[]{:S(2)}) collective-permute-start(f32[2,256,256]{2,1,0:T(8,128)} %bitcast.10), channel_id=1, source_target_pairs={{0,1},{1,0},{2,3},{3,2},{4,5},{5,4},{6,7},{7,6},{8,9},{9,8},{10,11... | collective-permute-start | bytes 1572872 | tf_op jit(solution)/shard_map/ppermute | solution.py:377
  3.7 1.2 %copy-done = f32[1,512,512]{2,1,0:T(8,128)S(1)} copy-done((f32[1,512,512]{2,1,0:T(8,128)S(1)}, f32[1,512,512]{2,1,0:T(8,128)}, u32[]{:S(2)}) %copy-start) | copy-done | bytes 1048600
  4.9 1.0 %copy-done.1 = f32[1,512,256]{2,1,0:T(8,128)S(1)} copy-done((f32[1,512,256]{2,1,0:T(8,128)S(1)}, f32[1,512,256]{2,1,0:T(8,128)}, u32[]{:S(2)}) %copy-start.1) | copy-done | bytes 524312
  5.9 14.8 %shard_map.76.g_ref.x_ref = f32[256,256]{1,0:T(8,128)S(1)} custom-call(s32[3,32]{1,0:T(4,128)S(1)} %copy-done.3, f32[512,512]{1,0:T(8,128)S(1)} %bitcast.8, f32[512,256]{1,0:T(8,128)S(1)} %bitcast.9), custom_call_target="tpu_custom_call" | custom-call | flops 8000000000 | bytes 4000000 | tf_op jit(solution)/shard_map/pallas_call | solution.py:365
  20.7 0.7 collective-permute-start
  21.4 0.0 copy-start.2
  21.5 1.6 %collective-permute-start.3 = (f32[2,256,256]{2,1,0:T(8,128)S(1)}, f32[2,256,256]{2,1,0:T(8,128)S(1)}, u32[]{:S(2)}, u32[]{:S(2)}) collective-permute-start(f32[2,256,256]{2,1,0:T(8,128)S(1)} %slice_bitcast_fusion.mine_ref), channel_id=1, source_target_pairs={{0,2},{1,3},{2,0},{3,1},{4,6},{5,7},{6,4},{7,5},{8,10},{9,11},{10,... | collective-permute-start | bytes 1572872 | tf_op jit(solution)/shard_map/ppermute | solution.py:377
  23.1 0.1 collective-permute-start.5
  23.1 5.4 %collective-permute-done.y_ref = f32[256,256]{1,0:T(8,128)S(1)} collective-permute-done((f32[256,256]{1,0:T(8,128)S(1)}, f32[256,256]{1,0:T(8,128)S(1)}, u32[]{:S(2)}, u32[]{:S(2)}) %collective-permute-start) | collective-permute-done | bytes 262176 | tf_op jit(solution)/shard_map/ppermute | solution.py:377
  28.6 0.0 collective-permute-done.1.theirs_ref
  28.6 3.8 %shard_map.78.g_ref.x_ref = f32[256,256]{1,0:T(8,128)S(1)} custom-call(s32[3,32]{1,0:T(4,128)S(1)} %copy-done.3, f32[256,256]{1,0:T(8,128)S(1)} %shard_map.76.g_ref.x_ref, f32[256,256]{1,0:T(8,128)S(1)} %collective-permute-done.y_ref, f32[2,256,256]{2,1,0:T(8,128)S(1)} %bitcast.11, f32[2,256,256]{2,1,0:T(8,128)S(1)} %collective-permute-done.1.theirs_ref), custom_call_target="tpu_custom_call" | custom-call | flops 1000000000 | bytes 4000000 | tf_op jit(solution)/shard_map/pallas_call | solution.py:365
  32.4 1.6 %collective-permute-start.2 = (f32[256,256]{1,0:T(8,128)S(1)}, f32[256,256]{1,0:T(8,128)S(1)}, u32[]{:S(2)}, u32[]{:S(2)}) collective-permute-start(f32[256,256]{1,0:T(8,128)S(1)} %shard_map.78.g_ref.x_ref), channel_id=1, source_target_pairs={{0,2},{1,3},{2,0},{3,1},{4,6},{5,7},{6,4},{7,5},{8,10},{9,11},{10,... | collective-permute-start | bytes 786440 | tf_op jit(solution)/shard_map/ppermute | solution.py:377
  34.0 4.6 %shard_map.77.before_ref = f32[256,256]{1,0:T(8,128)S(1)} custom-call(f32[256,256]{1,0:T(8,128)S(1)} %shard_map.76.g_ref.x_ref), custom_call_target="tpu_custom_call" | custom-call | flops 4000000000 | bytes 4000000 | tf_op jit(solution)/shard_map/pallas_call | solution.py:365
  38.6 0.0 collective-permute-done.3.theirs_ref
  38.6 1.9 %collective-permute-done.2.y_ref = f32[256,256]{1,0:T(8,128)S(1)} collective-permute-done((f32[256,256]{1,0:T(8,128)S(1)}, f32[256,256]{1,0:T(8,128)S(1)}, u32[]{:S(2)}, u32[]{:S(2)}) %collective-permute-start.2) | collective-permute-done | bytes 262176 | tf_op jit(solution)/shard_map/ppermute | solution.py:377
  40.5 3.7 %shard_map.80.g_ref = f32[256,256]{1,0:T(8,128)S(1)} custom-call(s32[3,32]{1,0:T(4,128)S(1)} %copy-done.3, f32[256,256]{1,0:T(8,128)S(1)} %shard_map.78.g_ref.x_ref, f32[256,256]{1,0:T(8,128)S(1)} %collective-permute-done.2.y_ref, f32[2,256,256]{2,1,0:T(8,128)S(1)} %slice_bitcast_fusion.mine_ref, f32[2,256,256]{2,1,0:T(8,128)S(1)} %collective-permute-done.3.theirs_ref), custom_call_target="tpu_custom_call" | custom-call | flops 1000000000 | bytes 4000000 | tf_op jit(solution)/shard_map/pallas_call | solution.py:365
  44.2 0.1 collective-permute-start.4
  44.3 6.5 %shard_map.79 = (f32[256,256]{1,0:T(8,128)}, f32[256,256]{1,0:T(8,128)S(1)}) custom-call(s32[3,32]{1,0:T(4,128)S(1)} %copy-done.3, f32[256,256]{1,0:T(8,128)S(1)} %shard_map.77.before_ref, f32[256,256]{1,0:T(8,128)S(1)} %shard_map.78.g_ref.x_ref), custom_call_target="tpu_custom_call" | custom-call | flops 4000000000 | bytes 4000000 | tf_op jit(solution)/shard_map/pallas_call | solution.py:365
  50.8 0.0 collective-permute-done.5.co_ref
  50.8 0.0 collective-permute-done.4.go_ref
  50.8 12.9 %shard_map.81 = (f32[256,256]{1,0:T(8,128)S(1)}, f32[256,256]{1,0:T(8,128)S(1)}, f32[2,256,256]{2,1,0:T(8,128)}) custom-call(s32[3,32]{1,0:T(4,128)S(1)} %copy-done.3, f32[256,256]{1,0:T(8,128)S(1)} %shard_map.80.g_ref, f32[256,256]{1,0:T(8,128)S(1)} %collective-permute-done.4.go_ref, f32[256,256]{1,0:T(8,128)S(1)} %slice_bitcast_fusion.1.c_ref, ...), custom_call_target="tpu_custom_call" | custom-call | flops 4000000000 | bytes 4000000 | tf_op jit(solution)/shard_map/pallas_call | solution.py:365
  63.7 0.5 collective-permute-start.6
  64.2 1.2 %collective-permute-done.6.ko_ref = f32[256,256]{1,0:T(8,128)S(1)} collective-permute-done((f32[256,256]{1,0:T(8,128)S(1)}, f32[256,256]{1,0:T(8,128)S(1)}, u32[]{:S(2)}, u32[]{:S(2)}) %collective-permute-start.6) | collective-permute-done | bytes 262176 | tf_op jit(solution)/shard_map/ppermute | solution.py:377
  65.4 2.0 %shard_map.82 = f32[512,512]{1,0:T(8,128)} custom-call(s32[3,32]{1,0:T(4,128)S(1)} %copy-done.3, f32[256,256]{1,0:T(8,128)S(1)} %get-tuple-element.15.k_ref, f32[256,256]{1,0:T(8,128)S(1)} %collective-permute-done.6.ko_ref, f32[256,256]{1,0:T(8,128)S(1)} %get-tuple-element.16.s_ref), custom_call_target="tpu_custom_call" | custom-call | flops 4000000000 | bytes 4000000 | tf_op jit(solution)/shard_map/pallas_call | solution.py:365
  (9 shorter events, 0.1 us)
Async XLA Ops:
  0.6 3.0 %copy-start.3 = (s32[3,32]{1,0:T(4,128)S(1)}, s32[3,32]{1,0:T(4,128)}, u32[]{:S(2)}) copy-start(s32[3,32]{1,0:T(4,128)} %rank_ref.11) | copy-start | bytes 1156
  0.6 27.9 %collective-permute-start.1 = (f32[2,256,256]{2,1,0:T(8,128)}, f32[2,256,256]{2,1,0:T(8,128)S(1)}, u32[]{:S(2)}, u32[]{:S(2)}) collective-permute-start(f32[2,256,256]{2,1,0:T(8,128)} %bitcast.10), channel_id=1, source_target_pairs={{0,1},{1,0},{2,3},{3,2},{4,5},{5,4},{6,7},{7,6},{8,9},{9,8},{10,11... | collective-permute-start | bytes 1572872 | tf_op jit(solution)/shard_map/ppermute | solution.py:377
  3.7 1.2 %copy-start = (f32[1,512,512]{2,1,0:T(8,128)S(1)}, f32[1,512,512]{2,1,0:T(8,128)}, u32[]{:S(2)}) copy-start(f32[1,512,512]{2,1,0:T(8,128)} %param.5) | copy-start | bytes 3145732
  4.9 1.0 %copy-start.1 = (f32[1,512,256]{2,1,0:T(8,128)S(1)}, f32[1,512,256]{2,1,0:T(8,128)}, u32[]{:S(2)}) copy-start(f32[1,512,256]{2,1,0:T(8,128)} %param.6) | copy-start | bytes 1572868
  5.9 15.5 %copy-start.4 = (f32[2,2,256,256]{3,2,1,0:T(8,128)S(1)}, f32[2,2,256,256]{3,2,1,0:T(8,128)}, u32[]{:S(2)}) copy-start(f32[2,2,256,256]{3,2,1,0:T(8,128)} %param.8) | copy-start | bytes 3145732
  20.7 7.8 %collective-permute-start = (f32[256,256]{1,0:T(8,128)S(1)}, f32[256,256]{1,0:T(8,128)S(1)}, u32[]{:S(2)}, u32[]{:S(2)}) collective-permute-start(f32[256,256]{1,0:T(8,128)S(1)} %shard_map.76.g_ref.x_ref), channel_id=1, source_target_pairs={{0,1},{1,0},{2,3},{3,2},{4,5},{5,4},{6,7},{7,6},{8,9},{9,8},{10,11... | collective-permute-start | bytes 786440 | tf_op jit(solution)/shard_map/ppermute | solution.py:377
  21.4 7.1 %copy-start.2 = (f32[1,2,256,256]{3,2,1,0:T(8,128)S(1)}, f32[1,2,256,256]{3,2,1,0:T(8,128)}, u32[]{:S(2)}) copy-start(f32[1,2,256,256]{3,2,1,0:T(8,128)} %param.7) | copy-start | bytes 1572868
  21.5 17.1 %collective-permute-start.3 = (f32[2,256,256]{2,1,0:T(8,128)S(1)}, f32[2,256,256]{2,1,0:T(8,128)S(1)}, u32[]{:S(2)}, u32[]{:S(2)}) collective-permute-start(f32[2,256,256]{2,1,0:T(8,128)S(1)} %slice_bitcast_fusion.mine_ref), channel_id=1, source_target_pairs={{0,2},{1,3},{2,0},{3,1},{4,6},{5,7},{6,4},{7,5},{8,10},{9,11},{10,... | collective-permute-start | bytes 1572872 | tf_op jit(solution)/shard_map/ppermute | solution.py:377
  23.1 27.7 %collective-permute-start.5 = (f32[256,256]{1,0:T(8,128)S(1)}, f32[256,256]{1,0:T(8,128)S(1)}, u32[]{:S(2)}, u32[]{:S(2)}) collective-permute-start(f32[256,256]{1,0:T(8,128)S(1)} %slice_bitcast_fusion.1.c_ref), channel_id=1, source_target_pairs={{0,4},{4,0},{8,12},{12,8},{16,20},{20,16},{24,28},{28,24},{1,5},{5... | collective-permute-start | bytes 786440 | tf_op jit(solution)/shard_map/ppermute | solution.py:377
  32.4 8.1 %collective-permute-start.2 = (f32[256,256]{1,0:T(8,128)S(1)}, f32[256,256]{1,0:T(8,128)S(1)}, u32[]{:S(2)}, u32[]{:S(2)}) collective-permute-start(f32[256,256]{1,0:T(8,128)S(1)} %shard_map.78.g_ref.x_ref), channel_id=1, source_target_pairs={{0,2},{1,3},{2,0},{3,1},{4,6},{5,7},{6,4},{7,5},{8,10},{9,11},{10,... | collective-permute-start | bytes 786440 | tf_op jit(solution)/shard_map/ppermute | solution.py:377
  44.2 6.6 %collective-permute-start.4 = (f32[256,256]{1,0:T(8,128)S(1)}, f32[256,256]{1,0:T(8,128)S(1)}, u32[]{:S(2)}, u32[]{:S(2)}) collective-permute-start(f32[256,256]{1,0:T(8,128)S(1)} %shard_map.80.g_ref), channel_id=1, source_target_pairs={{0,4},{4,0},{8,12},{12,8},{16,20},{20,16},{24,28},{28,24},{1,5},{5... | collective-permute-start | bytes 786440 | tf_op jit(solution)/shard_map/ppermute | solution.py:377
  63.7 1.7 %collective-permute-start.6 = (f32[256,256]{1,0:T(8,128)S(1)}, f32[256,256]{1,0:T(8,128)S(1)}, u32[]{:S(2)}, u32[]{:S(2)}) collective-permute-start(f32[256,256]{1,0:T(8,128)S(1)} %get-tuple-element.15.k_ref), channel_id=1, source_target_pairs={{0,4},{4,0},{8,12},{12,8},{16,20},{20,16},{24,28},{28,24},{1,5},{5... | collective-permute-start | bytes 786440 | tf_op jit(solution)/shard_map/ppermute | solution.py:377

commit v4 on v3

--- a/solution.py
+++ b/solution.py
@@ -40,7 +40,7 @@
 
 def total(terms):
     while len(terms) > 1:
-        terms = [a + b for a, b in zip(terms[::2], terms[1::2])]
+        terms = [a + b for a, b in zip(terms[::2], terms[1::2])] + terms[len(terms) // 2 * 2 :]
     return terms[0]
 
 
@@ -167,6 +167,121 @@
     lax.fori_loop(0, tiles, step, 0)
 
 
+def segment_col(x, c):
+    at = iota(x.shape, 1) // PANEL * PANEL + c
+    return jnp.take_along_axis(x, at, axis=1, mode="promise_in_bounds")
+
+
+def base_pass(a_ref, start, out):
+    groups = PANEL // SUB
+    sub = iota((SUB, LANES), 0)
+    lane = iota((SUB, LANES), 1)
+    segment, spot = lane // PANEL, lane % PANEL
+    rows = []
+    for g in range(groups):
+        row = jnp.zeros((SUB, LANES), jnp.float32)
+        for b in range(LANES // PANEL):
+            part = a_ref[start + b * PANEL + g * SUB : start + b * PANEL + (g + 1) * SUB, start : start + LANES]
+            row = jnp.where(segment == b, part, row)
+        rows.append(row)
+    for s in range(groups):
+        c0 = s * SUB
+        cols = [segment_col(rows[s], c0 + j) for j in range(SUB)]
+        other = {g: [segment_col(rows[g], c0 + j) for j in range(SUB)] for g in range(groups) if g != s}
+        piv = rows[s]
+        inv = 1.0 / row_of(cols[0], 0)
+        yield
+        for j in range(SUB):
+            here = spot == c0 + j
+            at = sub == j
+            line = row_of(piv, j)
+            mult = jnp.where(at, -1.0, cols[j])
+            now = inv
+            if j + 1 < SUB:
+                i = j + 1
+                inv = 1.0 / (row_of(cols[i], i) - (row_of(cols[i], j) * now) * row_of(cols[j], i))
+            line = jnp.where(here, 1.0, line)
+            piv = jnp.where(at | here, 0.0, piv) - mult * (line * now)
+            for i in range(j + 1, SUB):
+                cols[i] = jnp.where(at, 0.0, cols[i]) - mult * (row_of(cols[i], j) * now)
+            yield
+        rows[s] = piv
+        spread = [row_of(piv, j) for j in range(SUB)]
+        inside = (spot >= c0) & (spot < c0 + SUB)
+        for g, mult in other.items():
+            rows[g] = jnp.where(inside, 0.0, rows[g]) - total([m * y for m, y in zip(mult, spread)])
+        yield
+    out.append(jnp.concatenate([jnp.where(segment == b, r, 0.0) for b in range(LANES // PANEL) for r in rows], axis=0))
+    yield
+
+
+def level_pass(a_ref, start, size, before, out, rests):
+    row, col = iota((LANES, LANES), 0), iota((LANES, LANES), 1)
+    across = (row // (2 * size) == col // (2 * size)) & (row // size != col // size)
+    couple = jnp.where(across, a_ref[start : start + LANES, start : start + LANES], 0.0)
+    split = thirds(before)
+    e = thirds(dot6(split, thirds(couple)))
+    yield
+    x = before - dot6(e, split)
+    power = thirds(dot3(e, e))
+    yield
+    x = x + dot3(power, thirds(x))
+    power = thirds(dot3(power, power))
+    yield
+    out.append(x + dot3(power, thirds(x)))
+    rests.append(bdot(power[0], power[0]))
+    yield
+
+
+def join_pass(a_ref, x, y, out_ref, rests):
+    b, xs, ys = thirds(a_ref[:LANES, LANES:]), thirds(x), thirds(y)
+    u = thirds(dot6(xs, b))
+    v = thirds(dot3(ys, b, nt=True))
+    yield
+    power = thirds(dot3(v, u))
+    yield
+    z = y + dot3(power, ys)
+    power = thirds(dot3(power, power))
+    yield
+    z = z + dot3(power, thirds(z))
+    power = thirds(dot3(power, power))
+    yield
+    z = z + dot3(power, thirds(z))
+    rests.append(bdot(power[0], power[0]))
+    yield
+    w = dot6(u, thirds(z))
+    yield
+    out_ref[:LANES, :LANES] = x + dot6(thirds(w), u, nt=True)
+    out_ref[:LANES, LANES:] = -w
+    out_ref[LANES:, :LANES] = -w.T
+    out_ref[LANES:, LANES:] = z
+    yield
+
+
+def invert_pair(a_ref, out_ref):
+    count, n = a_ref.shape[0], a_ref.shape[1]
+    spots = [(i, t * LANES) for i in range(count) for t in range(n // LANES)]
+    found = [[] for _ in spots]
+    rests = []
+    together([base_pass(a_ref.at[i], at, f) for (i, at), f in zip(spots, found)])
+    size = PANEL
+    while size < LANES:
+        together([level_pass(a_ref.at[i], at, size, f[-1], f, rests) for (i, at), f in zip(spots, found)])
+        size = 2 * size
+    together([join_pass(a_ref.at[i], found[2 * i][-1], found[2 * i + 1][-1], out_ref.at[i], rests) for i in range(count)])
+    rest = total([r * r for r in rests])
+
+    @pl.when(jnp.logical_not(jnp.sum(rest) <= TOLERANCE * TOLERANCE))
+    def _():
+        out_ref[...] = a_ref[...]
+
+        def direct(i, carry):
+            eliminate([out_ref.at[i]])
+            return carry
+
+        lax.fori_loop(0, count, direct, 0)
+
+
 def unit_rest(n, rank):
     return jnp.where((iota((n, n), 0) == iota((n, n), 1)) & (iota((n, n), 0) >= rank), 1.0, 0.0)
 
@@ -231,7 +346,7 @@
         z = z + dot3(power, thirds(z))
     z_ref[...] = z
 
-    @pl.when(square_sum(raised) > TOLERANCE)
+    @pl.when(jnp.logical_not(square_sum(raised) <= TOLERANCE))
     def _():
         slow_dot(p_ref, x_ref, s_ref)
         slow_dot(q_ref, s_ref, y_ref)
@@ -265,17 +380,31 @@
     return g + dot6(thirds(turned), thirds(work[0][...]))
 
 
-def leaf_kernel(rank_ref, m_ref, v_ref, g_ref, x_ref, y_ref, s_ref, *work):
+def leaf_kernel(rank_ref, m_ref, v_ref, g_ref, a_ref, xy_ref, vv_ref, sem, s_ref, *work):
     n = g_ref.shape[0]
+    moves = [
+        (m_ref.at[:n, :n], a_ref.at[0]),
+        (m_ref.at[n:, n:], a_ref.at[1]),
+        (m_ref.at[:n, n:], s_ref),
+        (v_ref, vv_ref),
+    ]
+    copies = [pltpu.make_async_copy(src, dst, sem.at[i]) for i, (src, dst) in enumerate(moves)]
+    for copy in copies:
+        copy.start()
     rank = rank_ref[0, place()]
     keep = iota((n, n), 1) < rank
-    x_ref[...] = m_ref[:n, :n]
-    y_ref[...] = m_ref[n:, n:]
-    s_ref[...] = m_ref[:n, n:]
-    eliminate([x_ref, y_ref])
-    px = jnp.where(keep, v_ref[:n, :], 0.0)
-    py = jnp.where(keep, v_ref[n:, :], 0.0)
-    g_ref[...] = combine(3, x_ref, y_ref, s_ref, px, py, g_ref, work) + unit_rest(n, rank)
+    copies[0].wait()
+    copies[1].wait()
+    if n == 2 * LANES:
+        invert_pair(a_ref, xy_ref)
+    else:
+        xy_ref[...] = a_ref[...]
+        eliminate([xy_ref.at[0], xy_ref.at[1]])
+    copies[2].wait()
+    copies[3].wait()
+    px = jnp.where(keep, vv_ref[:n, :], 0.0)
+    py = jnp.where(keep, vv_ref[n:, :], 0.0)
+    g_ref[...] = combine(3, xy_ref.at[0], xy_ref.at[1], s_ref, px, py, g_ref, work) + unit_rest(n, rank)
 
 
 def merge_kernel(depth, rank_ref, x_ref, y_ref, mine_ref, theirs_ref, g_ref, s_ref, *work):
@@ -359,15 +488,15 @@
     f_ref[n:, n:] = factor_of(n, jnp.where(pick, ko_ref[...], k_ref[...]))
 
 
-def call(kernel, outs, n, scratch, *arrays, ranks=None, flops=10**9):
+def call(kernel, outs, n, scratch, *arrays, ranks=None, flops=10**9, held=(), space=pltpu.VMEM):
     vmem = pl.BlockSpec(memory_space=pltpu.VMEM)
     lead = [] if ranks is None else [pl.BlockSpec(memory_space=pltpu.SMEM)]
     return pl.pallas_call(
         kernel,
         out_shape=[jax.ShapeDtypeStruct(shape, jnp.float32) for shape in outs],
-        in_specs=lead + [vmem] * len(arrays),
+        in_specs=lead + [pl.BlockSpec(memory_space=space)] * len(arrays),
         out_specs=[vmem] * len(outs),
-        scratch_shapes=[pltpu.VMEM((n, n), jnp.float32)] * scratch,
+        scratch_shapes=[*held, *[pltpu.VMEM((n, n), jnp.float32)] * scratch],
         compiler_params=pltpu.CompilerParams(vmem_limit_bytes=GRANT),
         cost_estimate=pl.CostEstimate(flops=flops, bytes_accessed=4 * 10**6, transcendentals=0),
     )(*([] if ranks is None else [ranks]), *arrays)
@@ -383,7 +512,10 @@
     square = (n, n)
     gens = [local_gens[0]]
     others = [partner(gens[0], "inner", 0)]
-    g = call(leaf_kernel, [square], n, 7, leaf_blocks[0], leaf_bases[0], ranks=node_ranks, flops=8 * 10**9)[0]
+    pair = pltpu.VMEM((2, n, n), jnp.float32)
+    held = (pair, pair, pltpu.VMEM((2 * n, n), jnp.float32), pltpu.SemaphoreType.DMA((4,)))
+    arrays = (leaf_blocks[0], leaf_bases[0])
+    g = call(leaf_kernel, [square], n, 5, *arrays, ranks=node_ranks, flops=8 * 10**9, held=held, space=pltpu.HBM)[0]
     g_other = partner(g, "inner", 0)
     g, chain_gens = lax.optimization_barrier((g, chain_gens))
     gens = gens + [chain_gens[d] for d in range(in_levels)]

time: 67.6 us -> 62 us (0.917)
  Pallas kernels: 48.3 us -> 42.6 us
    pallas_call x7, Pallas kernels: 48.3 us -> 42.6 us  [call(): pl.pallas_call(kernel, out_shape=[jax.ShapeDtypeStruct(shape, jnp.float32...]
  transfers between devices with their start and end apart: 7 -> 7, of which waited for: 3 -> 3; matrix products, arithmetic and copies ran while one was open for 0% -> 0% of each run, Pallas kernels for 50% -> 45%
where the time goes in v4:
time: 62 us; the launch traced here: 61.8 us
  Pallas kernels  42.6 us (69%)
  waiting for transfers between devices  8.73 us (14%)
  starting transfers between devices  7.51 us (12%)
  local copies, waits for them, and re-layouts  2.33 us (4%)
  between operations  0.71 us (1%)
    pallas_call x7, Pallas kernels, call(): pl.pallas_call(kernel, out_shape=[jax.ShapeDtypeStruct(shape, jnp.float32...  42.6 us
    ppermute x7, waiting for transfers between devices, partner(): lax.ppermute(x, axis, [(i, i ^ 1 << bit) for i in range(lax.axis_size(axi...  8.73 us
    ppermute x7, starting transfers between devices, partner(): lax.ppermute(x, axis, [(i, i ^ 1 << bit) for i in range(lax.axis_size(axi...  7.51 us
    unnamed x10, local copies, waits for them, and re-layouts  2.28 us
  transfers between devices with their start and end apart: 7, of which 3 were waited for; matrix products, arithmetic and copies ran while one was open for 0% of the time, Pallas kernels for 45%

profile of v4, /device:TPU:0, one launch (start us, length us, event | category | flops | bytes accessed | tf_op | source)
XLA Modules:
  0.0 61.8 jit_solution(3660026640756994917)
XLA Ops:
  0.6 3.0 %collective-permute-start.1 = (f32[2,256,256]{2,1,0:T(8,128)}, f32[2,256,256]{2,1,0:T(8,128)S(1)}, u32[]{:S(2)}, u32[]{:S(2)}) collective-permute-start(f32[2,256,256]{2,1,0:T(8,128)} %bitcast.10), channel_id=1, source_target_pairs={{0,1},{1,0},{2,3},{3,2},{4,5},{5,4},{6,7},{7,6},{8,9},{9,8},{10,11... | collective-permute-start | bytes 1572872 | tf_op jit(solution)/shard_map/ppermute | solution.py:506
  3.7 1.2 %copy-done = f32[1,512,512]{2,1,0:T(8,128)S(1)} copy-done((f32[1,512,512]{2,1,0:T(8,128)S(1)}, f32[1,512,512]{2,1,0:T(8,128)}, u32[]{:S(2)}) %copy-start) | copy-done | bytes 1048600
  4.9 1.0 %copy-done.1 = f32[1,512,256]{2,1,0:T(8,128)S(1)} copy-done((f32[1,512,256]{2,1,0:T(8,128)S(1)}, f32[1,512,256]{2,1,0:T(8,128)}, u32[]{:S(2)}) %copy-start.1) | copy-done | bytes 524312
  5.9 9.0 %shard_map.76.g_ref.x_ref = f32[256,256]{1,0:T(8,128)S(1)} custom-call(s32[3,32]{1,0:T(4,128)S(1)} %copy-done.3, f32[512,512]{1,0:T(8,128)S(1)} %bitcast.8, f32[512,256]{1,0:T(8,128)S(1)} %bitcast.9), custom_call_target="tpu_custom_call" | custom-call | flops 8000000000 | bytes 4000000 | tf_op jit(solution)/shard_map/pallas_call | solution.py:494
  14.9 0.7 %collective-permute-start = (f32[256,256]{1,0:T(8,128)S(1)}, f32[256,256]{1,0:T(8,128)S(1)}, u32[]{:S(2)}, u32[]{:S(2)}) collective-permute-start(f32[256,256]{1,0:T(8,128)S(1)} %shard_map.76.g_ref.x_ref), channel_id=1, source_target_pairs={{0,1},{1,0},{2,3},{3,2},{4,5},{5,4},{6,7},{7,6},{8,9},{9,8},{10,11... | collective-permute-start | bytes 786440 | tf_op jit(solution)/shard_map/ppermute | solution.py:506
  15.6 0.0 copy-start.2
  15.7 1.6 %collective-permute-start.3 = (f32[2,256,256]{2,1,0:T(8,128)S(1)}, f32[2,256,256]{2,1,0:T(8,128)S(1)}, u32[]{:S(2)}, u32[]{:S(2)}) collective-permute-start(f32[2,256,256]{2,1,0:T(8,128)S(1)} %slice_bitcast_fusion.mine_ref), channel_id=1, source_target_pairs={{0,2},{1,3},{2,0},{3,1},{4,6},{5,7},{6,4},{7,5},{8,10},{9,11},{10,... | collective-permute-start | bytes 1572872 | tf_op jit(solution)/shard_map/ppermute | solution.py:506
  17.3 0.1 collective-permute-start.5
  17.3 5.4 %collective-permute-done.y_ref = f32[256,256]{1,0:T(8,128)S(1)} collective-permute-done((f32[256,256]{1,0:T(8,128)S(1)}, f32[256,256]{1,0:T(8,128)S(1)}, u32[]{:S(2)}, u32[]{:S(2)}) %collective-permute-start) | collective-permute-done | bytes 262176 | tf_op jit(solution)/shard_map/ppermute | solution.py:506
  22.8 0.0 collective-permute-done.1.theirs_ref
  22.8 3.7 %shard_map.78.g_ref.x_ref = f32[256,256]{1,0:T(8,128)S(1)} custom-call(s32[3,32]{1,0:T(4,128)S(1)} %copy-done.3, f32[256,256]{1,0:T(8,128)S(1)} %shard_map.76.g_ref.x_ref, f32[256,256]{1,0:T(8,128)S(1)} %collective-permute-done.y_ref, f32[2,256,256]{2,1,0:T(8,128)S(1)} %bitcast.11, f32[2,256,256]{2,1,0:T(8,128)S(1)} %collective-permute-done.1.theirs_ref), custom_call_target="tpu_custom_call" | custom-call | flops 1000000000 | bytes 4000000 | tf_op jit(solution)/shard_map/pallas_call | solution.py:494
  26.4 1.6 %collective-permute-start.2 = (f32[256,256]{1,0:T(8,128)S(1)}, f32[256,256]{1,0:T(8,128)S(1)}, u32[]{:S(2)}, u32[]{:S(2)}) collective-permute-start(f32[256,256]{1,0:T(8,128)S(1)} %shard_map.78.g_ref.x_ref), channel_id=1, source_target_pairs={{0,2},{1,3},{2,0},{3,1},{4,6},{5,7},{6,4},{7,5},{8,10},{9,11},{10,... | collective-permute-start | bytes 786440 | tf_op jit(solution)/shard_map/ppermute | solution.py:506
  28.0 4.6 %shard_map.77.before_ref = f32[256,256]{1,0:T(8,128)S(1)} custom-call(f32[256,256]{1,0:T(8,128)S(1)} %shard_map.76.g_ref.x_ref), custom_call_target="tpu_custom_call" | custom-call | flops 4000000000 | bytes 4000000 | tf_op jit(solution)/shard_map/pallas_call | solution.py:494
  32.6 0.0 collective-permute-done.3.theirs_ref
  32.6 2.1 %collective-permute-done.2.y_ref = f32[256,256]{1,0:T(8,128)S(1)} collective-permute-done((f32[256,256]{1,0:T(8,128)S(1)}, f32[256,256]{1,0:T(8,128)S(1)}, u32[]{:S(2)}, u32[]{:S(2)}) %collective-permute-start.2) | collective-permute-done | bytes 262176 | tf_op jit(solution)/shard_map/ppermute | solution.py:506
  34.7 3.9 %shard_map.80.g_ref = f32[256,256]{1,0:T(8,128)S(1)} custom-call(s32[3,32]{1,0:T(4,128)S(1)} %copy-done.3, f32[256,256]{1,0:T(8,128)S(1)} %shard_map.78.g_ref.x_ref, f32[256,256]{1,0:T(8,128)S(1)} %collective-permute-done.2.y_ref, f32[2,256,256]{2,1,0:T(8,128)S(1)} %slice_bitcast_fusion.mine_ref, f32[2,256,256]{2,1,0:T(8,128)S(1)} %collective-permute-done.3.theirs_ref), custom_call_target="tpu_custom_call" | custom-call | flops 1000000000 | bytes 4000000 | tf_op jit(solution)/shard_map/pallas_call | solution.py:494
  38.6 0.1 collective-permute-start.4
  38.7 6.5 %shard_map.79 = (f32[256,256]{1,0:T(8,128)}, f32[256,256]{1,0:T(8,128)S(1)}) custom-call(s32[3,32]{1,0:T(4,128)S(1)} %copy-done.3, f32[256,256]{1,0:T(8,128)S(1)} %shard_map.77.before_ref, f32[256,256]{1,0:T(8,128)S(1)} %shard_map.78.g_ref.x_ref), custom_call_target="tpu_custom_call" | custom-call | flops 4000000000 | bytes 4000000 | tf_op jit(solution)/shard_map/pallas_call | solution.py:494
  45.2 0.0 collective-permute-done.5.co_ref
  45.2 0.0 collective-permute-done.4.go_ref
  45.2 13.0 %shard_map.81 = (f32[256,256]{1,0:T(8,128)S(1)}, f32[256,256]{1,0:T(8,128)S(1)}, f32[2,256,256]{2,1,0:T(8,128)}) custom-call(s32[3,32]{1,0:T(4,128)S(1)} %copy-done.3, f32[256,256]{1,0:T(8,128)S(1)} %shard_map.80.g_ref, f32[256,256]{1,0:T(8,128)S(1)} %collective-permute-done.4.go_ref, f32[256,256]{1,0:T(8,128)S(1)} %slice_bitcast_fusion.1.c_ref, ...), custom_call_target="tpu_custom_call" | custom-call | flops 4000000000 | bytes 4000000 | tf_op jit(solution)/shard_map/pallas_call | solution.py:494
  58.2 0.5 collective-permute-start.6
  58.7 1.2 %collective-permute-done.6.ko_ref = f32[256,256]{1,0:T(8,128)S(1)} collective-permute-done((f32[256,256]{1,0:T(8,128)S(1)}, f32[256,256]{1,0:T(8,128)S(1)}, u32[]{:S(2)}, u32[]{:S(2)}) %collective-permute-start.6) | collective-permute-done | bytes 262176 | tf_op jit(solution)/shard_map/ppermute | solution.py:506
  59.8 2.0 %shard_map.82 = f32[512,512]{1,0:T(8,128)} custom-call(s32[3,32]{1,0:T(4,128)S(1)} %copy-done.3, f32[256,256]{1,0:T(8,128)S(1)} %get-tuple-element.15.k_ref, f32[256,256]{1,0:T(8,128)S(1)} %collective-permute-done.6.ko_ref, f32[256,256]{1,0:T(8,128)S(1)} %get-tuple-element.16.s_ref), custom_call_target="tpu_custom_call" | custom-call | flops 4000000000 | bytes 4000000 | tf_op jit(solution)/shard_map/pallas_call | solution.py:494
  (9 shorter events, 0.1 us)
Async XLA Ops:
  0.6 3.0 %copy-start.3 = (s32[3,32]{1,0:T(4,128)S(1)}, s32[3,32]{1,0:T(4,128)}, u32[]{:S(2)}) copy-start(s32[3,32]{1,0:T(4,128)} %rank_ref.11) | copy-start | bytes 1156
  0.6 22.1 %collective-permute-start.1 = (f32[2,256,256]{2,1,0:T(8,128)}, f32[2,256,256]{2,1,0:T(8,128)S(1)}, u32[]{:S(2)}, u32[]{:S(2)}) collective-permute-start(f32[2,256,256]{2,1,0:T(8,128)} %bitcast.10), channel_id=1, source_target_pairs={{0,1},{1,0},{2,3},{3,2},{4,5},{5,4},{6,7},{7,6},{8,9},{9,8},{10,11... | collective-permute-start | bytes 1572872 | tf_op jit(solution)/shard_map/ppermute | solution.py:506
  3.7 1.2 %copy-start = (f32[1,512,512]{2,1,0:T(8,128)S(1)}, f32[1,512,512]{2,1,0:T(8,128)}, u32[]{:S(2)}) copy-start(f32[1,512,512]{2,1,0:T(8,128)} %param.5) | copy-start | bytes 3145732
  4.9 1.0 %copy-start.1 = (f32[1,512,256]{2,1,0:T(8,128)S(1)}, f32[1,512,256]{2,1,0:T(8,128)}, u32[]{:S(2)}) copy-start(f32[1,512,256]{2,1,0:T(8,128)} %param.6) | copy-start | bytes 1572868
  5.9 9.7 %copy-start.4 = (f32[2,2,256,256]{3,2,1,0:T(8,128)S(1)}, f32[2,2,256,256]{3,2,1,0:T(8,128)}, u32[]{:S(2)}) copy-start(f32[2,2,256,256]{3,2,1,0:T(8,128)} %param.8) | copy-start | bytes 3145732
  14.9 7.8 %collective-permute-start = (f32[256,256]{1,0:T(8,128)S(1)}, f32[256,256]{1,0:T(8,128)S(1)}, u32[]{:S(2)}, u32[]{:S(2)}) collective-permute-start(f32[256,256]{1,0:T(8,128)S(1)} %shard_map.76.g_ref.x_ref), channel_id=1, source_target_pairs={{0,1},{1,0},{2,3},{3,2},{4,5},{5,4},{6,7},{7,6},{8,9},{9,8},{10,11... | collective-permute-start | bytes 786440 | tf_op jit(solution)/shard_map/ppermute | solution.py:506
  15.6 7.1 %copy-start.2 = (f32[1,2,256,256]{3,2,1,0:T(8,128)S(1)}, f32[1,2,256,256]{3,2,1,0:T(8,128)}, u32[]{:S(2)}) copy-start(f32[1,2,256,256]{3,2,1,0:T(8,128)} %param.7) | copy-start | bytes 1572868
  15.7 16.9 %collective-permute-start.3 = (f32[2,256,256]{2,1,0:T(8,128)S(1)}, f32[2,256,256]{2,1,0:T(8,128)S(1)}, u32[]{:S(2)}, u32[]{:S(2)}) collective-permute-start(f32[2,256,256]{2,1,0:T(8,128)S(1)} %slice_bitcast_fusion.mine_ref), channel_id=1, source_target_pairs={{0,2},{1,3},{2,0},{3,1},{4,6},{5,7},{6,4},{7,5},{8,10},{9,11},{10,... | collective-permute-start | bytes 1572872 | tf_op jit(solution)/shard_map/ppermute | solution.py:506
  17.3 28.0 %collective-permute-start.5 = (f32[256,256]{1,0:T(8,128)S(1)}, f32[256,256]{1,0:T(8,128)S(1)}, u32[]{:S(2)}, u32[]{:S(2)}) collective-permute-start(f32[256,256]{1,0:T(8,128)S(1)} %slice_bitcast_fusion.1.c_ref), channel_id=1, source_target_pairs={{0,4},{4,0},{8,12},{12,8},{16,20},{20,16},{24,28},{28,24},{1,5},{5... | collective-permute-start | bytes 786440 | tf_op jit(solution)/shard_map/ppermute | solution.py:506
  26.4 8.3 %collective-permute-start.2 = (f32[256,256]{1,0:T(8,128)S(1)}, f32[256,256]{1,0:T(8,128)S(1)}, u32[]{:S(2)}, u32[]{:S(2)}) collective-permute-start(f32[256,256]{1,0:T(8,128)S(1)} %shard_map.78.g_ref.x_ref), channel_id=1, source_target_pairs={{0,2},{1,3},{2,0},{3,1},{4,6},{5,7},{6,4},{7,5},{8,10},{9,11},{10,... | collective-permute-start | bytes 786440 | tf_op jit(solution)/shard_map/ppermute | solution.py:506
  38.6 6.6 %collective-permute-start.4 = (f32[256,256]{1,0:T(8,128)S(1)}, f32[256,256]{1,0:T(8,128)S(1)}, u32[]{:S(2)}, u32[]{:S(2)}) collective-permute-start(f32[256,256]{1,0:T(8,128)S(1)} %shard_map.80.g_ref), channel_id=1, source_target_pairs={{0,4},{4,0},{8,12},{12,8},{16,20},{20,16},{24,28},{28,24},{1,5},{5... | collective-permute-start | bytes 786440 | tf_op jit(solution)/shard_map/ppermute | solution.py:506
  58.2 1.7 %collective-permute-start.6 = (f32[256,256]{1,0:T(8,128)S(1)}, f32[256,256]{1,0:T(8,128)S(1)}, u32[]{:S(2)}, u32[]{:S(2)}) collective-permute-start(f32[256,256]{1,0:T(8,128)S(1)} %get-tuple-element.15.k_ref), channel_id=1, source_target_pairs={{0,4},{4,0},{8,12},{12,8},{16,20},{20,16},{24,28},{28,24},{1,5},{5... | collective-permute-start | bytes 786440 | tf_op jit(solution)/shard_map/ppermute | solution.py:506

commit v5 on v4

--- a/solution.py
+++ b/solution.py
@@ -12,7 +12,9 @@
 PANEL = 32
 TOLERANCE = 4e-6
 MOST = 40
+LOWEST = -3.4e38
 GRANT = 20 * 2**20
+WHOLE = 66_700_000
 HIGH = lax.Precision.HIGHEST
 
 
@@ -307,13 +309,17 @@
     axis = 1 if nt else 0
     small = product(jnp.concatenate([a2, a1, a3], axis=1), jnp.concatenate([b2, b3, b1], axis=axis), nt)
     large = product(jnp.concatenate([a2, a1, a1], axis=1), jnp.concatenate([b1, b2, b1], axis=axis), nt)
-    return small + large
+    return apart(small) + large
 
 
 def dot3(a, b, nt=False):
     axis = 1 if nt else 0
     small = product(jnp.concatenate([a[1], a[0]], axis=1), jnp.concatenate([b[0], b[1]], axis=axis), nt)
-    return small + product(a[0], b[0], nt)
+    return apart(small) + product(a[0], b[0], nt)
+
+
+def apart(x):
+    return jnp.maximum(x, LOWEST) if x.shape[0] > LANES else x
 
 
 def slow_dot(out_ref, a_ref, b_ref, dims=((1,), (0,)), add=False):
@@ -332,12 +338,15 @@
     return jnp.sum(x * x)
 
 
-def neumann(steps, x_ref, y_ref, s_ref, z, hold_ref, work):
-    z_ref, p_ref, q_ref, w_ref = work
+def first_power(x_ref, y_ref, s_ref):
     s = thirds(s_ref[...])
     a = dot3(thirds(x_ref[...]), s)
     u = dot3(s, thirds(y_ref[...]))
-    power = thirds(dot3(thirds(a), thirds(u), nt=True))
+    return thirds(dot3(thirds(a), thirds(u), nt=True))
+
+
+def neumann(steps, power, x_ref, y_ref, s_ref, z, hold_ref, work):
+    z_ref, p_ref, q_ref, w_ref = work
     hold_ref[...] = z
     z = z + dot3(power, thirds(z))
     for _ in range(steps - 1):
@@ -372,11 +381,12 @@
 def combine(steps, x_ref, y_ref, s_ref, px, py, g_ref, work):
     py3 = thirds(py)
     t = thirds(dot6(thirds(y_ref[...]), py3))
+    power = first_power(x_ref, y_ref, s_ref)
     y = px - dot6(thirds(s_ref[...]), t)
     z = dot6(thirds(x_ref[...]), thirds(y))
     g = dot6(thirds(py.T), t)
     turned = y.T
-    neumann(steps, x_ref, y_ref, s_ref, z, g_ref, work)
+    neumann(steps, power, x_ref, y_ref, s_ref, z, g_ref, work)
     return g + dot6(thirds(turned), thirds(work[0][...]))
 
 
@@ -464,7 +474,7 @@
     cb = jnp.where(pick, co_ref[...], c_ref[...])
     s_ref[...] = both(n, rb, ra, ca.T + cb)
     h_ref[...] = before_ref[...]
-    neumann(2, b_ref, a_ref, s_ref, b_ref[...], l_ref, work)
+    neumann(2, first_power(b_ref, a_ref, s_ref), b_ref, a_ref, s_ref, b_ref[...], l_ref, work)
     turned = thirds(s_ref[...])
     back = dot6(thirds(dot6(turned, thirds(a_ref[...]))), turned, nt=True)
     l_ref[...] = jnp.where(pick, 0.0, back)
@@ -488,7 +498,7 @@
     f_ref[n:, n:] = factor_of(n, jnp.where(pick, ko_ref[...], k_ref[...]))
 
 
-def call(kernel, outs, n, scratch, *arrays, ranks=None, flops=10**9, held=(), space=pltpu.VMEM):
+def call(kernel, outs, n, scratch, *arrays, ranks=None, flops=10**9, held=(), space=pltpu.VMEM, grant=GRANT):
     vmem = pl.BlockSpec(memory_space=pltpu.VMEM)
     lead = [] if ranks is None else [pl.BlockSpec(memory_space=pltpu.SMEM)]
     return pl.pallas_call(
@@ -497,7 +507,7 @@
         in_specs=lead + [pl.BlockSpec(memory_space=space)] * len(arrays),
         out_specs=[vmem] * len(outs),
         scratch_shapes=[*held, *[pltpu.VMEM((n, n), jnp.float32)] * scratch],
-        compiler_params=pltpu.CompilerParams(vmem_limit_bytes=GRANT),
+        compiler_params=pltpu.CompilerParams(vmem_limit_bytes=grant),
         cost_estimate=pl.CostEstimate(flops=flops, bytes_accessed=4 * 10**6, transcendentals=0),
     )(*([] if ranks is None else [ranks]), *arrays)
 
@@ -515,7 +525,7 @@
     pair = pltpu.VMEM((2, n, n), jnp.float32)
     held = (pair, pair, pltpu.VMEM((2 * n, n), jnp.float32), pltpu.SemaphoreType.DMA((4,)))
     arrays = (leaf_blocks[0], leaf_bases[0])
-    g = call(leaf_kernel, [square], n, 5, *arrays, ranks=node_ranks, flops=8 * 10**9, held=held, space=pltpu.HBM)[0]
+    g = call(leaf_kernel, [square], n, 5, *arrays, ranks=node_ranks, flops=8 * 10**9, held=held, space=pltpu.HBM, grant=WHOLE)[0]
     g_other = partner(g, "inner", 0)
     g, chain_gens = lax.optimization_barrier((g, chain_gens))
     gens = gens + [chain_gens[d] for d in range(in_levels)]

time: 62 us -> 60.9 us (0.982)
  waiting for transfers between devices: 8.73 us -> 7.34 us
    unnamed x10 -> x6, local copies, waits for them, and re-layouts: 2.28 us -> 0.02 us
    ppermute x7, waiting for transfers between devices: 8.73 us -> 7.34 us  [partner(): lax.ppermute(x, axis, [(i, i ^ 1 << bit) for i in range(lax.axis_size(axi...]
    squeeze x1, local copies, waits for them, and re-layouts: 0.03 us -> 1.12 us  [steps(): gens = gens + [chain_gens[d] for d in range(in_levels)]]
    squeeze x1, local copies, waits for them, and re-layouts: 0.02 us -> 0.97 us  [steps(): couple = gens[in_levels][1]]
  transfers between devices with their start and end apart: 7 -> 7, of which waited for: 3 -> 3; matrix products, arithmetic and copies ran while one was open for 0% -> 3% of each run, Pallas kernels for 45% -> 46%
where the time goes in v5:
time: 60.9 us; the launch traced here: 60.6 us
  Pallas kernels  43 us (71%)
  starting transfers between devices  7.43 us (12%)
  waiting for transfers between devices  7.34 us (12%)
  local copies, waits for them, and re-layouts  2.1 us (3%)
  between operations  0.72 us (1%)
    pallas_call x7, Pallas kernels, call(): pl.pallas_call(kernel, out_shape=[jax.ShapeDtypeStruct(shape, jnp.float32...  43 us
    ppermute x7, starting transfers between devices, partner(): lax.ppermute(x, axis, [(i, i ^ 1 << bit) for i in range(lax.axis_size(axi...  7.43 us
    ppermute x7, waiting for transfers between devices, partner(): lax.ppermute(x, axis, [(i, i ^ 1 << bit) for i in range(lax.axis_size(axi...  7.34 us
  transfers between devices with their start and end apart: 7, of which 3 were waited for; matrix products, arithmetic and copies ran while one was open for 3% of the time, Pallas kernels for 46%

profile of v5, /device:TPU:0, one launch (start us, length us, event | category | flops | bytes accessed | tf_op | source)
XLA Modules:
  0.0 60.6 jit_solution(5642928336900560066)
XLA Ops:
  0.6 3.0 %collective-permute-start.1 = (f32[2,256,256]{2,1,0:T(8,128)}, f32[2,256,256]{2,1,0:T(8,128)}, u32[]{:S(2)}, u32[]{:S(2)}) collective-permute-start(f32[2,256,256]{2,1,0:T(8,128)} %bitcast.8), channel_id=1, source_target_pairs={{0,1},{1,0},{2,3},{3,2},{4,5},{5,4},{6,7},{7,6},{8,9},{9,8},{10,11... | collective-permute-start | bytes 1572872 | tf_op jit(solution)/shard_map/ppermute | solution.py:516
  3.7 10.1 %shard_map.76.g_ref.x_ref = f32[256,256]{1,0:T(8,128)} custom-call(s32[3,32]{1,0:T(4,128)} %rank_ref.11, f32[512,512]{1,0:T(8,128)} %bitcast.10, f32[512,256]{1,0:T(8,128)} %bitcast.11), custom_call_target="tpu_custom_call" | custom-call | flops 8000000000 | bytes 4000000 | tf_op jit(solution)/shard_map/pallas_call | solution.py:504
  13.8 0.1 collective-permute-start
  13.8 0.0 copy-start.2
  13.9 1.1 %slice_bitcast_fusion.mine_ref = f32[2,256,256]{2,1,0:T(8,128)S(1)} fusion(f32[2,2,256,256]{3,2,1,0:T(8,128)} %param.8), kind=kLoop, calls=%fused_computation | loop fusion | bytes 1048576 | tf_op jit(solution)/shard_map/squeeze | solution.py:531
  15.0 0.0 copy-start
  15.0 2.1 %collective-permute-start.3 = (f32[2,256,256]{2,1,0:T(8,128)S(1)}, f32[2,256,256]{2,1,0:T(8,128)S(1)}, u32[]{:S(2)}, u32[]{:S(2)}) collective-permute-start(f32[2,256,256]{2,1,0:T(8,128)S(1)} %slice_bitcast_fusion.mine_ref), channel_id=1, source_target_pairs={{0,2},{1,3},{2,0},{3,1},{4,6},{5,7},{6,4},{7,5},{8,10},{9,11},{10,... | collective-permute-start | bytes 1572872 | tf_op jit(solution)/shard_map/ppermute | solution.py:516
  17.1 1.0 %slice_bitcast_fusion.1.c_ref = f32[256,256]{1,0:T(8,128)S(1)} fusion(f32[2,2,256,256]{3,2,1,0:T(8,128)} %param.8), kind=kLoop, calls=%fused_computation.1 | loop fusion | bytes 524288 | tf_op jit(solution)/shard_map/squeeze | solution.py:532
  18.0 0.1 collective-permute-start.5
  18.1 3.7 %collective-permute-done.y_ref = f32[256,256]{1,0:T(8,128)S(1)} collective-permute-done((f32[256,256]{1,0:T(8,128)}, f32[256,256]{1,0:T(8,128)S(1)}, u32[]{:S(2)}, u32[]{:S(2)}) %collective-permute-start) | collective-permute-done | bytes 262176 | tf_op jit(solution)/shard_map/ppermute | solution.py:516
  21.8 0.0 collective-permute-done.1.theirs_ref
  21.8 3.6 %shard_map.78.g_ref.x_ref = f32[256,256]{1,0:T(8,128)S(1)} custom-call(s32[3,32]{1,0:T(4,128)S(1)} %copy-done.2, f32[256,256]{1,0:T(8,128)S(1)} %copy-done.1, f32[256,256]{1,0:T(8,128)S(1)} %collective-permute-done.y_ref, f32[2,256,256]{2,1,0:T(8,128)S(1)} %bitcast.9, f32[2,256,256]{2,1,0:T(8,128)} %collective-permute-done.1.theirs_ref), custom_call_target="tpu_custom_call" | custom-call | flops 1000000000 | bytes 4000000 | tf_op jit(solution)/shard_map/pallas_call | solution.py:504
  25.4 1.6 %collective-permute-start.2 = (f32[256,256]{1,0:T(8,128)S(1)}, f32[256,256]{1,0:T(8,128)S(1)}, u32[]{:S(2)}, u32[]{:S(2)}) collective-permute-start(f32[256,256]{1,0:T(8,128)S(1)} %shard_map.78.g_ref.x_ref), channel_id=1, source_target_pairs={{0,2},{1,3},{2,0},{3,1},{4,6},{5,7},{6,4},{7,5},{8,10},{9,11},{10,... | collective-permute-start | bytes 786440 | tf_op jit(solution)/shard_map/ppermute | solution.py:516
  27.0 4.6 %shard_map.77.before_ref = f32[256,256]{1,0:T(8,128)S(1)} custom-call(f32[256,256]{1,0:T(8,128)S(1)} %copy-done.1), custom_call_target="tpu_custom_call" | custom-call | flops 4000000000 | bytes 4000000 | tf_op jit(solution)/shard_map/pallas_call | solution.py:504
  31.5 0.0 collective-permute-done.3.theirs_ref
  31.6 2.5 %collective-permute-done.2.y_ref = f32[256,256]{1,0:T(8,128)S(1)} collective-permute-done((f32[256,256]{1,0:T(8,128)S(1)}, f32[256,256]{1,0:T(8,128)S(1)}, u32[]{:S(2)}, u32[]{:S(2)}) %collective-permute-start.2) | collective-permute-done | bytes 262176 | tf_op jit(solution)/shard_map/ppermute | solution.py:516
  34.1 3.3 %shard_map.80.g_ref = f32[256,256]{1,0:T(8,128)S(1)} custom-call(s32[3,32]{1,0:T(4,128)S(1)} %copy-done.2, f32[256,256]{1,0:T(8,128)S(1)} %shard_map.78.g_ref.x_ref, f32[256,256]{1,0:T(8,128)S(1)} %collective-permute-done.2.y_ref, f32[2,256,256]{2,1,0:T(8,128)S(1)} %slice_bitcast_fusion.mine_ref, f32[2,256,256]{2,1,0:T(8,128)S(1)} %collective-permute-done.3.theirs_ref), custom_call_target="tpu_custom_call" | custom-call | flops 1000000000 | bytes 4000000 | tf_op jit(solution)/shard_map/pallas_call | solution.py:504
  37.3 0.1 collective-permute-start.4
  37.4 6.5 %shard_map.79 = (f32[256,256]{1,0:T(8,128)}, f32[256,256]{1,0:T(8,128)S(1)}) custom-call(s32[3,32]{1,0:T(4,128)S(1)} %copy-done.2, f32[256,256]{1,0:T(8,128)S(1)} %shard_map.77.before_ref, f32[256,256]{1,0:T(8,128)S(1)} %shard_map.78.g_ref.x_ref), custom_call_target="tpu_custom_call" | custom-call | flops 4000000000 | bytes 4000000 | tf_op jit(solution)/shard_map/pallas_call | solution.py:504
  44.0 0.0 collective-permute-done.5.co_ref
  44.0 13.0 %shard_map.81 = (f32[256,256]{1,0:T(8,128)S(1)}, f32[256,256]{1,0:T(8,128)S(1)}, f32[2,256,256]{2,1,0:T(8,128)}) custom-call(s32[3,32]{1,0:T(4,128)S(1)} %copy-done.2, f32[256,256]{1,0:T(8,128)S(1)} %shard_map.80.g_ref, f32[256,256]{1,0:T(8,128)S(1)} %collective-permute-done.4.go_ref, f32[256,256]{1,0:T(8,128)S(1)} %slice_bitcast_fusion.1.c_ref, ...), custom_call_target="tpu_custom_call" | custom-call | flops 4000000000 | bytes 4000000 | tf_op jit(solution)/shard_map/pallas_call | solution.py:504
  56.9 0.5 collective-permute-start.6
  57.4 1.2 %collective-permute-done.6.ko_ref = f32[256,256]{1,0:T(8,128)S(1)} collective-permute-done((f32[256,256]{1,0:T(8,128)S(1)}, f32[256,256]{1,0:T(8,128)S(1)}, u32[]{:S(2)}, u32[]{:S(2)}) %collective-permute-start.6) | collective-permute-done | bytes 262176 | tf_op jit(solution)/shard_map/ppermute | solution.py:516
  58.6 2.0 %shard_map.82 = f32[512,512]{1,0:T(8,128)} custom-call(s32[3,32]{1,0:T(4,128)S(1)} %copy-done.2, f32[256,256]{1,0:T(8,128)S(1)} %get-tuple-element.15.k_ref, f32[256,256]{1,0:T(8,128)S(1)} %collective-permute-done.6.ko_ref, f32[256,256]{1,0:T(8,128)S(1)} %get-tuple-element.16.s_ref), custom_call_target="tpu_custom_call" | custom-call | flops 4000000000 | bytes 4000000 | tf_op jit(solution)/shard_map/pallas_call | solution.py:504
  (5 shorter events, 0.0 us)
Async XLA Ops:
  0.6 21.2 %collective-permute-start.1 = (f32[2,256,256]{2,1,0:T(8,128)}, f32[2,256,256]{2,1,0:T(8,128)}, u32[]{:S(2)}, u32[]{:S(2)}) collective-permute-start(f32[2,256,256]{2,1,0:T(8,128)} %bitcast.8), channel_id=1, source_target_pairs={{0,1},{1,0},{2,3},{3,2},{4,5},{5,4},{6,7},{7,6},{8,9},{9,8},{10,11... | collective-permute-start | bytes 1572872 | tf_op jit(solution)/shard_map/ppermute | solution.py:516
  13.8 8.0 %collective-permute-start = (f32[256,256]{1,0:T(8,128)}, f32[256,256]{1,0:T(8,128)S(1)}, u32[]{:S(2)}, u32[]{:S(2)}) collective-permute-start(f32[256,256]{1,0:T(8,128)} %shard_map.76.g_ref.x_ref), channel_id=1, source_target_pairs={{0,1},{1,0},{2,3},{3,2},{4,5},{5,4},{6,7},{7,6},{8,9},{9,8},{10,11... | collective-permute-start | bytes 786440 | tf_op jit(solution)/shard_map/ppermute | solution.py:516
  13.8 8.0 %copy-start.1 = (f32[256,256]{1,0:T(8,128)S(1)}, f32[256,256]{1,0:T(8,128)}, u32[]{:S(2)}) copy-start(f32[256,256]{1,0:T(8,128)} %shard_map.76.g_ref.x_ref) | copy-start | bytes 786436
  13.8 8.0 %copy-start.2 = (s32[3,32]{1,0:T(4,128)S(1)}, s32[3,32]{1,0:T(4,128)}, u32[]{:S(2)}) copy-start(s32[3,32]{1,0:T(4,128)} %rank_ref.11) | copy-start | bytes 1156
  15.0 6.8 %copy-start = (f32[1,2,256,256]{3,2,1,0:T(8,128)S(1)}, f32[1,2,256,256]{3,2,1,0:T(8,128)}, u32[]{:S(2)}) copy-start(f32[1,2,256,256]{3,2,1,0:T(8,128)} %param.7) | copy-start | bytes 1572868
  15.0 16.6 %collective-permute-start.3 = (f32[2,256,256]{2,1,0:T(8,128)S(1)}, f32[2,256,256]{2,1,0:T(8,128)S(1)}, u32[]{:S(2)}, u32[]{:S(2)}) collective-permute-start(f32[2,256,256]{2,1,0:T(8,128)S(1)} %slice_bitcast_fusion.mine_ref), channel_id=1, source_target_pairs={{0,2},{1,3},{2,0},{3,1},{4,6},{5,7},{6,4},{7,5},{8,10},{9,11},{10,... | collective-permute-start | bytes 1572872 | tf_op jit(solution)/shard_map/ppermute | solution.py:516
  18.0 25.9 %collective-permute-start.5 = (f32[256,256]{1,0:T(8,128)S(1)}, f32[256,256]{1,0:T(8,128)S(1)}, u32[]{:S(2)}, u32[]{:S(2)}) collective-permute-start(f32[256,256]{1,0:T(8,128)S(1)} %slice_bitcast_fusion.1.c_ref), channel_id=1, source_target_pairs={{0,4},{4,0},{8,12},{12,8},{16,20},{20,16},{24,28},{28,24},{1,5},{5... | collective-permute-start | bytes 786440 | tf_op jit(solution)/shard_map/ppermute | solution.py:516
  25.4 8.7 %collective-permute-start.2 = (f32[256,256]{1,0:T(8,128)S(1)}, f32[256,256]{1,0:T(8,128)S(1)}, u32[]{:S(2)}, u32[]{:S(2)}) collective-permute-start(f32[256,256]{1,0:T(8,128)S(1)} %shard_map.78.g_ref.x_ref), channel_id=1, source_target_pairs={{0,2},{1,3},{2,0},{3,1},{4,6},{5,7},{6,4},{7,5},{8,10},{9,11},{10,... | collective-permute-start | bytes 786440 | tf_op jit(solution)/shard_map/ppermute | solution.py:516
  37.3 6.6 %collective-permute-start.4 = (f32[256,256]{1,0:T(8,128)S(1)}, f32[256,256]{1,0:T(8,128)S(1)}, u32[]{:S(2)}, u32[]{:S(2)}) collective-permute-start(f32[256,256]{1,0:T(8,128)S(1)} %shard_map.80.g_ref), channel_id=1, source_target_pairs={{0,4},{4,0},{8,12},{12,8},{16,20},{20,16},{24,28},{28,24},{1,5},{5... | collective-permute-start | bytes 786440 | tf_op jit(solution)/shard_map/ppermute | solution.py:516
  56.9 1.7 %collective-permute-start.6 = (f32[256,256]{1,0:T(8,128)S(1)}, f32[256,256]{1,0:T(8,128)S(1)}, u32[]{:S(2)}, u32[]{:S(2)}) collective-permute-start(f32[256,256]{1,0:T(8,128)S(1)} %get-tuple-element.15.k_ref), channel_id=1, source_target_pairs={{0,4},{4,0},{8,12},{12,8},{16,20},{20,16},{24,28},{28,24},{1,5},{5... | collective-permute-start | bytes 786440 | tf_op jit(solution)/shard_map/ppermute | solution.py:516
